TPU v7x, 256 devices: a whole 4x4x8 slice. The times are simulated.
256 devices in a mesh: sec: 32 (over z, y), depth: 4 (over x), segment: 2 (over core).
Axes of the slice: x: 4, y: 4, z: 8, core: 2. Of those that a mesh axis runs over, the one named last changes fastest.
Arguments:
- fields: float32 [2, 9, 64, 64, 128], P('segment', None, 'sec', 'depth'), may hold values from -6 to 6
- block_ids: int32 [2, 64, 64, 128], P('segment', 'sec', 'depth'), may hold values from 0 to 15
- buoyancy: float32 [16], replicated, may hold values from 0.5 to 1
- lame_lambda: float32 [16], replicated, may hold values from 0.2 to 0.6
- lame_mu: float32 [16], replicated, may hold values from 0.1 to 0.3
- moments: float32 [6, 131072], P(None, ('sec', 'depth')), may hold values from -12 to 12
- moment_owner: int32 [131072, 1], P(('sec', 'depth')), may hold values from 0 to 31; in each aligned block of 1024 rows (0 to 1023, 1024 to 2047, ...) at most 64 rows name the same one
- moment_cells: int32 [131072], P(('sec', 'depth')), may hold values from 0 to 4095
- drm_rows: int32 [262144], P(('sec', 'depth')), may hold values from 0 to 4095
Outputs:
- final_fields: float32 [2, 9, 64, 64, 128], P('segment', None, 'sec', 'depth')
Inputs may be any that keep to these rules, and one draw needn't show every extreme that they name: `moment_owner`: in the entries of one section and slab at most 64 name the same section, a bound that some block reaches of them.
All inputs are finite; a program needn't handle non-finite values.
Results may differ from a plain program's by a relative error of at most 0.00002.
Values sent between devices are 32-bit elements; how exact they have to be, the bound alone decides.
A program may use at most 64 MiB of HBM per device.

v0:
```python
import jax
import jax.numpy as jnp
from jax import lax
from jax.sharding import PartitionSpec as P

STEPS = 4


HALF_STEP = 0.5


def passed_along(block, axis, distance):
    devices = range(lax.axis_size(axis))
    route = [(i - distance, i) for i in devices if i - distance in devices]
    return lax.ppermute(block, axis, route)


def lookup(block_ids, table):
    result = jnp.zeros(block_ids.shape, jnp.float32)
    for entry in range(table.shape[0]):
        result = result + jnp.where(block_ids == entry, table[entry], jnp.float32(0.0))
    return result


def back_diff(field, before_rim, axis):
    count = field.shape[axis]
    before = jnp.concatenate([before_rim, lax.slice_in_dim(field, 0, count - 1, axis=axis)], axis)
    return field - before


def fore_diff(field, after_rim, axis):
    count = field.shape[axis]
    after = jnp.concatenate([lax.slice_in_dim(field, 1, count, axis=axis), after_rim], axis)
    return after - field


def stress_rims(state):
    xplane = jnp.stack([state[:, 3, -1:], state[:, 8, -1:], state[:, 7, -1:]], axis=1)
    zplane = jnp.stack([state[:, 7, :, -1:], state[:, 6, :, -1:], state[:, 5, :, -1:]], axis=1)
    x_rims = passed_along(xplane, "sec", 1)
    z_rims = passed_along(zplane, "depth", 1)
    return (x_rims, z_rims)


def velocity_rims(newv):
    xplane = newv[:, :, :1]
    zplane = newv[:, :, :, :1]
    x_rims = passed_along(xplane, "sec", -1)
    z_rims = passed_along(zplane, "depth", -1)
    return (x_rims, z_rims)


def couple(newv, oldv, rows_here):
    shape_one = newv.shape[1:]
    increment = (newv[0] - oldv[0]).reshape(3, -1)[:, rows_here]
    arrived = passed_along(increment, "segment", 1)
    basin = newv[0].reshape(3, -1).at[:, rows_here].add(arrived)
    return basin.reshape((1,) + shape_one)


def advance(state, buoy, lam, shear, rows_here):
    x_rims, z_rims = stress_rims(state)
    vx, vy, vz = (state[:, 0], state[:, 1], state[:, 2])
    sxx, syy, szz, syz, sxz, sxy = (state[:, k] for k in range(3, 9))
    y_zero = jnp.zeros_like(sxx[..., :1])
    nvx = vx + HALF_STEP * buoy * (
        back_diff(sxx, x_rims[:, 0], 1)
        + back_diff(sxy, y_zero, 3)
        + back_diff(sxz, z_rims[:, 0], 2)
    )
    nvy = vy + HALF_STEP * buoy * (
        back_diff(sxy, x_rims[:, 1], 1)
        + back_diff(syy, y_zero, 3)
        + back_diff(syz, z_rims[:, 1], 2)
    )
    nvz = vz + HALF_STEP * buoy * (
        back_diff(sxz, x_rims[:, 2], 1)
        + back_diff(syz, y_zero, 3)
        + back_diff(szz, z_rims[:, 2], 2)
    )
    newv = couple(jnp.stack([nvx, nvy, nvz], axis=1), state[:, :3], rows_here)
    vx_rims, vz_rims = velocity_rims(newv)
    vx, vy, vz = (newv[:, 0], newv[:, 1], newv[:, 2])
    exx = fore_diff(vx, vx_rims[:, 0], 1)
    eyy = fore_diff(vy, y_zero, 3)
    ezz = fore_diff(vz, vz_rims[:, 2], 2)
    trace = exx + eyy + ezz
    sxx = sxx + HALF_STEP * (lam * trace + 2.0 * shear * exx)
    syy = syy + HALF_STEP * (lam * trace + 2.0 * shear * eyy)
    szz = szz + HALF_STEP * (lam * trace + 2.0 * shear * ezz)
    syz = syz + HALF_STEP * shear * (fore_diff(vy, vz_rims[:, 1], 2) + fore_diff(vz, y_zero, 3))
    sxz = sxz + HALF_STEP * shear * (
        fore_diff(vx, vz_rims[:, 0], 2) + fore_diff(vz, vx_rims[:, 2], 1)
    )
    sxy = sxy + HALF_STEP * shear * (fore_diff(vx, y_zero, 3) + fore_diff(vy, vx_rims[:, 1], 1))
    return jnp.stack([vx, vy, vz, sxx, syy, szz, syz, sxz, sxy], axis=1)


def on_device(
    fields, block_ids, buoyancy, lame_lambda, lame_mu, moments, moment_owner, moment_cells, drm_rows
):
    my_section = lax.axis_index("sec")
    segment_pos = lax.axis_index("segment")
    width_x, width_z, width_y = (fields.shape[2], fields.shape[3], fields.shape[4])
    cells_here = width_x * width_z * width_y
    all_moments, all_owner, all_cells = (
        lax.all_gather(moments, "sec", axis=1, tiled=True),
        lax.all_gather(moment_owner, "sec", axis=0, tiled=True),
        lax.all_gather(moment_cells, "sec", axis=0, tiled=True),
    )
    values = all_moments
    places = jnp.where(all_owner[:, 0] == my_section, all_cells, cells_here)
    values = values * (segment_pos == 0).astype(jnp.float32)
    stress = fields[0, 3:].reshape(6, -1).at[:, places].add(values, mode="drop")
    state = jnp.concatenate(
        [fields[:, :3], stress.reshape(1, 6, width_x, width_z, width_y)], axis=1
    )
    block_here = block_ids[:, None]
    block_here = block_here[:, 0]
    buoy = lookup(block_here, buoyancy)
    lam = lookup(block_here, lame_lambda)
    shear = lookup(block_here, lame_mu)
    for step in range(STEPS):
        state = advance(state, buoy, lam, shear, drm_rows)
    return state


def solution(mesh):
    in_specs = (
        P("segment", None, "sec", "depth", None),
        P("segment", "sec", "depth", None),
        P(),
        P(),
        P(),
        P(None, ("sec", "depth")),
        P(("sec", "depth"), None),
        P(("sec", "depth")),
        P(("sec", "depth")),
    )
    out_specs = P("segment", None, "sec", "depth", None)
    return jax.shard_map(
        on_device, mesh=mesh, in_specs=in_specs, out_specs=out_specs, check_vma=False
    )
```

profile of v0, /device:TPU:31, one launch (start us, length us, event | category | flops | bytes accessed | tf_op | source)
XLA Modules:
  0.0 600.2 jit_solution(15526155525644759450)
XLA Ops:
  0.0 41.3 %all_gather.11 = f32[6,32768]{1,0:T(8,128)S(1)} all-gather(f32[6,1024]{1,0:T(8,128)} %param.14), channel_id=1, replica_groups=mesh['sec'=32,'depth'=4,'segment'=2] {'sec'}, dimensions={1}, use_global_device_ids=true | all-gather | bytes 811008 | tf_op jit(solution)/shard_map/all_gather | solution.py:107
  41.5 8.9 %copy.799 = f32[32768,6]{1,0:T(8,128)} copy(f32[32768,6]{0,1:T(8,128)S(1)} %multiply_bitcast_fusion) | data formatting | bytes 1572864 | tf_op jit(solution)/shard_map/mul | solution.py:113
  50.4 31.5 %all_gather.9 = s32[32768,1]{0,1:T(1,128)S(1)} all-gather(s32[1024,1]{0,1:T(1,128)S(1)} %copy-done.12), channel_id=1, replica_groups=mesh['sec'=32,'depth'=4,'segment'=2] {'sec'}, dimensions={0}, use_global_device_ids=true | all-gather | bytes 135168 | tf_op jit(solution)/shard_map/all_gather | solution.py:108
  81.8 32.4 %all_gather.10 = s32[32768]{0:T(1024)S(1)} all-gather(s32[1024]{0:T(1024)S(1)} %copy-done.13), channel_id=1, replica_groups=mesh['sec'=32,'depth'=4,'segment'=2] {'sec'}, dimensions={0}, use_global_device_ids=true | all-gather | bytes 135168 | tf_op jit(solution)/shard_map/all_gather | solution.py:109
  115.3 175.0 %scatter_fusion = f32[6,4096]{0,1:T(8,128)S(1)} fusion(f32[6,4096]{0,1:T(8,128)S(1)} %bitcast.376, s32[32768]{0:T(1024)S(1)} %compare_select_fusion, f32[32768,6]{1,0:T(8,128)} %copy.799), kind=kCustom, calls=%fused_computation.4 | custom fusion | flops 196608 | bytes 2490368 | tf_op jit(solution)/shard_map/scatter-add | solution.py:114
  297.6 3.5 collective-permute-start
  301.1 7.3 %fusion.93 = (f32[1,1,2,16,128]{1,4,3,2,0:T(8,128)}, f32[1,1,2,16,128]{1,4,3,2,0:T(8,128)}, f32[1,1,2,16,128]{1,4,3,2,0:T(8,128)}, f32[1,1,2,16,128]{1,4,3,2,0:T...) fusion(f32[1,6,2,16,128]{1,4,3,2,0:T(8,128)S(1)} %bitcast.379), kind=kLoop, calls=%fused_computation.240 | loop fusion | bytes 196608 | tf_op jit(solution)/shard_map/slice | solution.py:64
  322.4 10.7 %fusion.3 = (f32[1,2,16,128]{3,2,1,0:T(8,128)S(1)}, f32[1,2,16,128]{3,2,1,0:T(8,128)S(1)}, pred[1,2,16,128]{3,2,1,0:T(8,128)(4,1)S(1)}, pred[1,2,16,128]{3,2,1,0...) fusion(f32[1,1,16,128]{3,2,1,0:T(8,128)S(1)} %slice.912, ...), kind=kLoop, calls=%fused_computation.29 | loop fusion | flops 233472 | bytes 229312 | tf_op jit(solution)/shard_map/add | solution.py:66
  337.0 7.0 %gather_fusion = f32[2048,3]{1,0:T(8,128)S(1)} fusion(f32[3,4096]{0,1:T(8,128)} %bitcast_subtract_fusion, s32[2048]{0:T(1024)S(1)} %get-tuple-element.103), kind=kCustom, calls=%fused_computation | custom fusion | bytes 57344 | tf_op jit(solution)/shard_map/gather | solution.py:55
  346.6 31.1 %collective-permute-done.2 = f32[3,2048]{1,0:T(4,128)S(1)} collective-permute-done((f32[3,2048]{1,0:T(4,128)S(1)}, f32[3,2048]{1,0:T(4,128)S(1)}, u32[]{:S(2)}, u32[]{:S(2)}) %collective-permute-start.2) | collective-permute-done | bytes 24608 | tf_op jit(solution)/shard_map/ppermute | solution.py:15
  378.0 12.2 %scatter_fusion.1 = f32[3,4096]{0,1:T(8,128)S(1)} fusion(f32[3,4096]{0,1:T(8,128)S(1)} %copy.807, s32[2048]{0:T(1024)S(1)} %get-tuple-element.104, f32[2048,3]{1,0:T(8,128)S(1)} %copy.808), kind=kCustom, calls=%fused_computation.5 | custom fusion | flops 6144 | bytes 81920 | tf_op jit(solution)/shard_map/scatter-add | solution.py:57
  390.4 4.3 collective-permute-start.4
  394.7 4.0 fusion.92
  408.2 4.5 collective-permute-done.3
  412.6 20.5 %multiply_add_fusion.6 = (f32[1,2,16,128]{3,2,1,0:T(8,128)S(1)}, f32[1,2,16,128]{3,2,1,0:T(8,128)S(1)}, f32[1,2,16,128]{3,2,1,0:T(8,128)S(1)}, f32[1,2,16,128]{3,2,1,0:T(8,128)S(1)}) fusion(f32[1,2,16,127]{3,2,1,0:T(8,128)S(1)} %slice.939, f32[1,1,2,16,128]{4,3,2,1,0:T(8,128)S(1)} %copy.875, f32[1,1,2,16,128]{4,3,2,1,0:T(8,128)S(1)} %copy.870, ...), kind=kLoop, calls=%fused_computation.178 | loop fusion | flops 307200 | bytes 245760 | tf_op jit(solution)/shard_map/add | solution.py:89
  444.5 7.2 %gather_fusion.1 = f32[2048,3]{1,0:T(8,128)S(1)} fusion(f32[3,4096]{0,1:T(8,128)} %sub.500, s32[2048]{0:T(1024)S(1)} %get-tuple-element.103), kind=kCustom, calls=%fused_computation.1 | custom fusion | bytes 57344 | tf_op jit(solution)/shard_map/gather | solution.py:55
  453.4 3.5 collective-permute-done.7
  457.2 12.2 %scatter_fusion.2 = f32[3,4096]{0,1:T(8,128)S(1)} fusion(f32[3,4096]{0,1:T(8,128)S(1)} %copy-done, s32[2048]{0:T(1024)S(1)} %get-tuple-element.104, f32[2048,3]{1,0:T(8,128)S(1)} %copy.821), kind=kCustom, calls=%fused_computation.6 | custom fusion | flops 6144 | bytes 81920 | tf_op jit(solution)/shard_map/scatter-add | solution.py:57
  469.6 4.3 collective-permute-start.9
  473.9 4.0 fusion.91
  487.1 4.7 collective-permute-done.8
  503.3 7.2 %gather_fusion.2 = f32[2048,3]{1,0:T(8,128)S(1)} fusion(f32[3,4096]{0,1:T(8,128)} %sub.519, s32[2048]{0:T(1024)S(1)} %get-tuple-element.103), kind=kCustom, calls=%fused_computation.2 | custom fusion | bytes 57344 | tf_op jit(solution)/shard_map/gather | solution.py:55
  512.3 3.2 collective-permute-done.12
  515.9 12.2 %scatter_fusion.3 = f32[3,4096]{0,1:T(8,128)S(1)} fusion(f32[3,4096]{0,1:T(8,128)S(1)} %copy-done.1, s32[2048]{0:T(1024)S(1)} %get-tuple-element.104, f32[2048,3]{1,0:T(8,128)S(1)} %copy.834), kind=kCustom, calls=%fused_computation.7 | custom fusion | flops 6144 | bytes 81920 | tf_op jit(solution)/shard_map/scatter-add | solution.py:57
  528.3 4.3 collective-permute-start.14
  532.5 4.0 fusion.90
  545.8 4.7 collective-permute-done.13
  562.0 7.2 %gather_fusion.3 = f32[2048,3]{1,0:T(8,128)S(1)} fusion(f32[3,4096]{0,1:T(8,128)} %sub.538, s32[2048]{0:T(1024)S(1)} %get-tuple-element.103), kind=kCustom, calls=%fused_computation.3 | custom fusion | bytes 57344 | tf_op jit(solution)/shard_map/gather | solution.py:55
  570.8 3.4 collective-permute-done.17
  574.6 12.2 %scatter_fusion.4 = f32[3,4096]{0,1:T(8,128)S(1)} fusion(f32[3,4096]{0,1:T(8,128)S(1)} %copy-done.2, s32[2048]{0:T(1024)S(1)} %get-tuple-element.104, f32[2048,3]{1,0:T(8,128)S(1)} %copy.847), kind=kCustom, calls=%fused_computation.8 | custom fusion | flops 6144 | bytes 81920 | tf_op jit(solution)/shard_map/scatter-add | solution.py:57
  587.6 4.3 collective-permute-start.19
  594.1 4.7 collective-permute-done.18
  (238 shorter events, 101.7 us)
Async XLA Ops:
  41.4 8.9 %copy-start.12 = (s32[1024,1]{0,1:T(1,128)S(1)}, s32[1024,1]{0,1:T(1,128)}, u32[]{:S(2)}) copy-start(s32[1024,1]{0,1:T(1,128)} %param.15) | copy-start | bytes 12292
  41.4 40.4 %copy-start.13 = (s32[1024]{0:T(1024)S(1)}, s32[1024]{0:T(1024)}, u32[]{:S(2)}) copy-start(s32[1024]{0:T(1024)} %param.16) | copy-start | bytes 12292
  41.4 72.8 %slice-start = ((f32[1,9,2,16,128]{4,3,2,1,0:T(8,128)}), f32[1,6,2,16,128]{4,3,2,1,0:T(8,128)S(1)}, s32[]{:S(2)}) async-start(f32[1,9,2,16,128]{4,3,2,1,0:T(8,128)} %param.9), calls=%async_computation | async-start | bytes 196608 | tf_op jit(solution)/shard_map/slice | solution.py:114
  290.8 31.6 %collective-permute-start.1 = (f32[1,3,2,1,128]{4,3,2,1,0:T(1,128)S(1)}, f32[1,3,2,1,128]{4,3,2,1,0:T(1,128)S(1)}, u32[]{:S(2)}, u32[]{:S(2)}) collective-permute-start(f32[1,3,2,1,128]{4,3,2,1,0:T(1,128)S(1)} %pad_maximum_fusion.8), channel_id=1, source_target_pairs={{0,2},{2,4},{4,6},{1,3},{3,5},{5,7},{8,10},{10,12},{12,14},{9,11},... | collective-permute-start | bytes 9224 | tf_op jit(solution)/shard_map/ppermute | solution.py:15
  297.5 10.9 %copy-start.6 = (f32[16]{0:T(128)S(1)}, f32[16]{0:T(128)}, u32[]{:S(2)}) copy-start(f32[16]{0:T(128)} %param.11) | copy-start | bytes 196
  297.5 11.6 %copy-start.11 = (s32[2048]{0:T(1024)S(1)}, s32[2048]{0:T(1024)}, u32[]{:S(2)}) copy-start(s32[2048]{0:T(1024)} %param.17) | copy-start | bytes 24580
  297.6 11.6 %copy-start.7 = (f32[16]{0:T(128)S(1)}, f32[16]{0:T(128)}, u32[]{:S(2)}) copy-start(f32[16]{0:T(128)} %param.12) | copy-start | bytes 196
  297.6 24.8 %collective-permute-start = (f32[1,3,1,16,128]{4,3,2,1,0:T(8,128)S(1)}, f32[1,3,1,16,128]{4,3,2,1,0:T(8,128)S(1)}, u32[]{:S(2)}, u32[]{:S(2)}) collective-permute-start(f32[1,3,1,16,128]{4,3,2,1,0:T(8,128)S(1)} %pad_maximum_fusion.4), channel_id=1, source_target_pairs={{0,8},{8,16},{16,24},{24,32},{32,40},{40,48},{48,56},{56,64},{64,7... | collective-permute-start | bytes 73736 | tf_op jit(solution)/shard_map/ppermute | solution.py:15
  309.9 4.6 copy-start.4
  315.1 4.6 copy-start.3
  333.9 12.0 %copy-start.8 = (f32[16]{0:T(128)S(1)}, f32[16]{0:T(128)}, u32[]{:S(2)}) copy-start(f32[16]{0:T(128)} %param.13) | copy-start | bytes 196
  344.4 33.3 %collective-permute-start.2 = (f32[3,2048]{1,0:T(4,128)S(1)}, f32[3,2048]{1,0:T(4,128)S(1)}, u32[]{:S(2)}, u32[]{:S(2)}) collective-permute-start(f32[3,2048]{1,0:T(4,128)S(1)} %copy.806), channel_id=1, source_target_pairs={{0,1},{2,3},{4,5},{6,7},{8,9},{10,11},{12,13},{14,15},{16,17},{18,... | collective-permute-start | bytes 73736 | tf_op jit(solution)/shard_map/ppermute | solution.py:15
  390.4 17.8 %collective-permute-start.4 = (f32[1,3,2,1,128]{4,2,3,1,0:T(2,128)S(1)}, f32[1,3,2,1,128]{4,2,3,1,0:T(2,128)S(1)}, u32[]{:S(2)}, u32[]{:S(2)}) collective-permute-start(f32[1,3,2,1,128]{4,2,3,1,0:T(2,128)S(1)} %copy.877), channel_id=1, source_target_pairs={{2,0},{4,2},{6,4},{3,1},{5,3},{7,5},{10,8},{12,10},{14,12},{11,9},... | collective-permute-start | bytes 9224 | tf_op jit(solution)/shard_map/ppermute | solution.py:15
  405.9 6.7 %collective-permute-start.3 = (f32[1,3,1,16,128]{4,3,2,1,0:T(8,128)S(1)}, f32[1,3,1,16,128]{4,3,2,1,0:T(8,128)S(1)}, u32[]{:S(2)}, u32[]{:S(2)}) collective-permute-start(f32[1,3,1,16,128]{4,3,2,1,0:T(8,128)S(1)} %copy.874), channel_id=1, source_target_pairs={{8,0},{16,8},{24,16},{32,24},{40,32},{48,40},{56,48},{64,56},{72,6... | collective-permute-start | bytes 73736 | tf_op jit(solution)/shard_map/ppermute | solution.py:15
  433.2 4.3 collective-permute-start.6
  434.6 4.6 collective-permute-start.5
  444.5 12.7 %copy-start = (f32[3,4096]{0,1:T(8,128)S(1)}, f32[3,4096]{0,1:T(8,128)}, u32[]{:S(2)}) copy-start(f32[3,4096]{0,1:T(8,128)} %copy.820) | copy-start | bytes 147460
  452.1 4.8 collective-permute-start.7
  469.6 17.5 %collective-permute-start.9 = (f32[1,3,2,1,128]{4,2,3,1,0:T(2,128)S(1)}, f32[1,3,2,1,128]{4,2,3,1,0:T(2,128)S(1)}, u32[]{:S(2)}, u32[]{:S(2)}) collective-permute-start(f32[1,3,2,1,128]{4,2,3,1,0:T(2,128)S(1)} %copy.885), channel_id=1, source_target_pairs={{2,0},{4,2},{6,4},{3,1},{5,3},{7,5},{10,8},{12,10},{14,12},{11,9},... | collective-permute-start | bytes 9224 | tf_op jit(solution)/shard_map/ppermute | solution.py:15
  485.2 6.7 %collective-permute-start.8 = (f32[1,3,1,16,128]{4,3,2,1,0:T(8,128)S(1)}, f32[1,3,1,16,128]{4,3,2,1,0:T(8,128)S(1)}, u32[]{:S(2)}, u32[]{:S(2)}) collective-permute-start(f32[1,3,1,16,128]{4,3,2,1,0:T(8,128)S(1)} %copy.882), channel_id=1, source_target_pairs={{8,0},{16,8},{24,16},{32,24},{40,32},{48,40},{56,48},{64,56},{72,6... | collective-permute-start | bytes 73736 | tf_op jit(solution)/shard_map/ppermute | solution.py:15
  492.0 4.3 collective-permute-start.11
  493.3 4.6 collective-permute-start.10
  503.3 12.6 %copy-start.1 = (f32[3,4096]{0,1:T(8,128)S(1)}, f32[3,4096]{0,1:T(8,128)}, u32[]{:S(2)}) copy-start(f32[3,4096]{0,1:T(8,128)} %copy.833) | copy-start | bytes 147460
  510.8 4.7 collective-permute-start.12
  528.3 17.5 %collective-permute-start.14 = (f32[1,3,2,1,128]{4,2,3,1,0:T(2,128)S(1)}, f32[1,3,2,1,128]{4,2,3,1,0:T(2,128)S(1)}, u32[]{:S(2)}, u32[]{:S(2)}) collective-permute-start(f32[1,3,2,1,128]{4,2,3,1,0:T(2,128)S(1)} %copy.893), channel_id=1, source_target_pairs={{2,0},{4,2},{6,4},{3,1},{5,3},{7,5},{10,8},{12,10},{14,12},{11,9},... | collective-permute-start | bytes 9224 | tf_op jit(solution)/shard_map/ppermute | solution.py:15
  543.8 6.7 %collective-permute-start.13 = (f32[1,3,1,16,128]{4,3,2,1,0:T(8,128)S(1)}, f32[1,3,1,16,128]{4,3,2,1,0:T(8,128)S(1)}, u32[]{:S(2)}, u32[]{:S(2)}) collective-permute-start(f32[1,3,1,16,128]{4,3,2,1,0:T(8,128)S(1)} %copy.890), channel_id=1, source_target_pairs={{8,0},{16,8},{24,16},{32,24},{40,32},{48,40},{56,48},{64,56},{72,6... | collective-permute-start | bytes 73736 | tf_op jit(solution)/shard_map/ppermute | solution.py:15
  550.6 4.3 collective-permute-start.16
  552.0 4.6 collective-permute-start.15
  562.0 12.6 %copy-start.2 = (f32[3,4096]{0,1:T(8,128)S(1)}, f32[3,4096]{0,1:T(8,128)}, u32[]{:S(2)}) copy-start(f32[3,4096]{0,1:T(8,128)} %copy.846) | copy-start | bytes 147460
  569.5 4.7 collective-permute-start.17
  587.6 6.5 %collective-permute-start.19 = (f32[1,3,2,1,128]{4,2,3,1,0:T(2,128)S(1)}, f32[1,3,2,1,128]{4,2,3,1,0:T(2,128)S(1)}, u32[]{:S(2)}, u32[]{:S(2)}) collective-permute-start(f32[1,3,2,1,128]{4,2,3,1,0:T(2,128)S(1)} %copy.897), channel_id=1, source_target_pairs={{2,0},{4,2},{6,4},{3,1},{5,3},{7,5},{10,8},{12,10},{14,12},{11,9},... | collective-permute-start | bytes 9224 | tf_op jit(solution)/shard_map/ppermute | solution.py:15
  592.1 6.7 %collective-permute-start.18 = (f32[1,3,1,16,128]{4,3,2,1,0:T(8,128)S(1)}, f32[1,3,1,16,128]{4,3,2,1,0:T(8,128)S(1)}, u32[]{:S(2)}, u32[]{:S(2)}) collective-permute-start(f32[1,3,1,16,128]{4,3,2,1,0:T(8,128)S(1)} %slice.1059), channel_id=1, source_target_pairs={{8,0},{16,8},{24,16},{32,24},{40,32},{48,40},{56,48},{64,56},{72,6... | collective-permute-start | bytes 73736 | tf_op jit(solution)/shard_map/ppermute | solution.py:15
  (4 other events, 8.9 us)
where the time goes:
time: 606 us; the launch traced here: 600 us
  other arithmetic  270 us (45%)
  local copies, waits for them, and re-layouts  111 us (18%)
  blocking collectives  105 us (17%)
  waiting for transfers between devices  67.7 us (11%)
  starting transfers between devices  45 us (7%)
    scatter-add x1, other arithmetic, on_device(): stress = fields[0, 3:].reshape(6, -1).at[:, places].add(values, mode='drop')  175 us
    ppermute x20, waiting for transfers between devices, passed_along(): return lax.ppermute(block, axis, route)  67.7 us
    scatter-add x4, other arithmetic, couple(): basin = newv[0].reshape(3, -1).at[:, rows_here].add(arrived)  49 us
    ppermute x20, starting transfers between devices, passed_along(): return lax.ppermute(block, axis, route)  45 us
    all_gather x1, blocking collectives, on_device(): lax.all_gather(moments, 'sec', axis=1, tiled=True)  41.3 us
    unnamed x57, local copies, waits for them, and re-layouts  36 us
    all_gather x1, blocking collectives, on_device(): lax.all_gather(moment_cells, 'sec', axis=0, tiled=True)  32.4 us
    all_gather x1, blocking collectives, on_device(): lax.all_gather(moment_owner, 'sec', axis=0, tiled=True)  31.5 us
  transfers between devices with their start and end apart: 20, of which 14 were waited for; matrix products, arithmetic and copies ran while one was open for 10% of the time, Pallas kernels for 0%

commit v1 on v0

v1 whole, which is shorter than its diff:
```python
import functools

import jax
import jax.numpy as jnp
from jax import lax
from jax.experimental import pallas as pl
from jax.experimental.pallas import tpu as pltpu
from jax.sharding import PartitionSpec as P

MESH = pl.DeviceIdType.MESH
CX, CZ, CY = 2, 16, 128
ENT, ROWS, CAP, BUCKETS = 1024, 2048, 64, 32
PX, RZ = CX + 4, 24
X0, Z0 = 2, 4
OWN_X = slice(X0, X0 + CX)
OWN_Z = slice(Z0, Z0 + CZ)
NEAR = tuple((dx, dz) for dx in (-1, 0, 1) for dz in (-1, 0, 1) if (dx, dz) != (0, 0))
NT = (((1,), (1,)), ((), ()))
BF16, F32, I32 = jnp.bfloat16, jnp.float32, jnp.int32


def split(value):
    high = value.astype(BF16).astype(F32)
    return high, value - high


def source_z(dz):
    return {-1: (0, 2), 0: (0, CZ), 1: (CZ - 2, 2)}[dz]


def target_z(dz):
    return {-1: Z0 + CZ, 0: Z0, 1: Z0 - 2}[dz]


def target_x(dx):
    return X0 - CX * dx


def in_range(sec, depth, n_sec, n_depth):
    ok_sec = jnp.logical_and(sec >= 0, sec < n_sec)
    ok_depth = jnp.logical_and(depth >= 0, depth < n_depth)
    return jnp.logical_and(ok_sec, ok_depth)


def fill_buckets(owner, cells, mom, bucket, lhs, rhs):
    owners = [owner[t:t + 1, :] for t in range(8)]
    row32 = lax.broadcasted_iota(I32, (BUCKETS, 128), 0)
    hot = [jnp.where(row32 == o, 1.0, 0.0) for o in owners]
    before = jnp.where(
        lax.broadcasted_iota(I32, (128, 256), 0) < lax.broadcasted_iota(I32, (128, 256), 1), 1.0, 0.0
    ).astype(BF16)
    counts = jnp.dot(jnp.concatenate(hot, 0).astype(BF16), before, preferred_element_type=F32)
    running = jnp.zeros((BUCKETS, 128), F32)
    row16 = lax.broadcasted_iota(I32, (16, 128), 0)
    row256 = lax.broadcasted_iota(I32, (256, 128), 0)
    for t in range(8):
        part = counts[t * BUCKETS:(t + 1) * BUCKETS]
        rank = jnp.sum(hot[t] * (part[:, :128] + running), axis=0, keepdims=True).astype(I32)
        running = running + part[:, 128:]
        cols = slice(t * 128, (t + 1) * 128)
        slot = (owners[t] & 1) * 128 + rank
        mine = row16 == (owners[t] >> 1)
        cell = cells[t:t + 1, :].astype(F32)
        for h in range(2):
            at = slice((2 * t + h) * 128, (2 * t + h + 1) * 128)
            rhs[:, at] = jnp.where(row256 == slot + h * CAP, 1.0, 0.0).astype(BF16)
            for j in range(4):
                value = mom[2 * j + h:2 * j + h + 1, cols] if j < 3 else cell
                high, low = split(value)
                lhs[j * 16:(j + 1) * 16, at] = jnp.where(mine, high, 0.0).astype(BF16)
                lhs[64 + j * 16:64 + (j + 1) * 16, at] = jnp.where(mine, low, 0.0).astype(BF16)
    sums = lax.dot_general(lhs[0:128, :], rhs[...], NT, preferred_element_type=F32)
    sums = sums[0:64] + sums[64:128]
    for j in range(4):
        for x in range(2):
            bucket[x * 16:(x + 1) * 16, j, :] = sums[j * 16:(j + 1) * 16, x * 128:(x + 1) * 128]


def place(cell):
    return (cell >> 7) & 15, ((cell >> 11) << 7) | (cell & 127)


def add_buckets(arrived, state, leaving, lhs, rhs):
    low_half = lax.broadcasted_iota(I32, (16, 128), 1) < CAP
    values, cell = [], None
    for j in range(4):
        rows = arrived[:, j, :]
        a, b = rows[0:16], rows[16:32]
        even = jnp.where(low_half, a, pltpu.roll(b, CAP, 1))
        if j < 3:
            values.append(even)
            values.append(jnp.where(low_half, pltpu.roll(a, CAP, 1), b))
        else:
            cell = even.astype(I32)
    z, lane = place(cell)
    parts = [split(value) for value in values]
    row16 = lax.broadcasted_iota(I32, (16, 128), 0)
    row256 = lax.broadcasted_iota(I32, (256, 128), 0)
    for t in range(16):
        at = slice(t * 128, (t + 1) * 128)
        mine = row16 == z[t:t + 1]
        rhs[:, at] = jnp.where(row256 == lane[t:t + 1], 1.0, 0.0).astype(BF16)
        for k, (high, low) in enumerate(parts):
            lhs[k * 16:(k + 1) * 16, at] = jnp.where(mine, high[t:t + 1], 0.0).astype(BF16)
            lhs[96 + k * 16:96 + (k + 1) * 16, at] = jnp.where(mine, low[t:t + 1], 0.0).astype(BF16)
    sums = lax.dot_general(lhs[...], rhs[...], NT, preferred_element_type=F32)
    sums = sums[0:96] + sums[96:192]
    for k in range(6):
        for x in range(CX):
            total = state[3 + k, X0 + x, OWN_Z, :] + sums[k * 16:(k + 1) * 16, x * 128:(x + 1) * 128]
            state[3 + k, X0 + x, OWN_Z, :] = total
            leaving[3 + k, x] = total


def count_rows(rows, counts, lhs, rhs):
    z, lane = place(rows[...])
    row16 = lax.broadcasted_iota(I32, (16, 128), 0)
    row256 = lax.broadcasted_iota(I32, (256, 128), 0)
    for t in range(16):
        at = slice(t * 128, (t + 1) * 128)
        lhs[0:16, at] = jnp.where(row16 == z[t:t + 1], 1.0, 0.0).astype(BF16)
        rhs[:, at] = jnp.where(row256 == lane[t:t + 1], 1.0, 0.0).astype(BF16)
    sums = lax.dot_general(lhs[0:16, :], rhs[...], NT, preferred_element_type=F32)
    for x in range(CX):
        counts[X0 + x, OWN_Z, :] = sums[:, x * 128:(x + 1) * 128]


def look_up(ids, tables, coefs):
    for p in range(PX):
        block = ids[p]
        values = [jnp.zeros((RZ, CY), F32) for _ in tables]
        for entry in range(16):
            here = block == entry
            values = [jnp.where(here, table[entry], v) for table, v in zip(tables, values)]
        for k, v in enumerate(values):
            coefs[k, p] = 0.5 * v


def y_before(f, first):
    return jnp.where(first, 0.0, pltpu.roll(f, 1, 1))


def y_after(f, last):
    return jnp.where(last, 0.0, pltpu.roll(f, CY - 1, 1))


def z_before(f):
    return pltpu.roll(f, 1, 0)


def z_after(f):
    return pltpu.roll(f, RZ - 1, 0)


def increments(state, coefs, p):
    first = lax.broadcasted_iota(I32, (RZ, CY), 1) == 0
    b = coefs[0, p]
    sxx, syy, szz, syz, sxz, sxy = (state[k, p] for k in range(3, 9))
    bxx, bxz, bxy = (state[k, p - 1] for k in (3, 7, 8))
    ix = b * ((sxx - bxx) + (sxy - y_before(sxy, first)) + (sxz - z_before(sxz)))
    iy = b * ((sxy - bxy) + (syy - y_before(syy, first)) + (syz - z_before(syz)))
    iz = b * ((sxz - bxz) + (syz - y_before(syz, first)) + (szz - z_before(szz)))
    return ix, iy, iz


def stress(state, coefs, p):
    last = lax.broadcasted_iota(I32, (RZ, CY), 1) == CY - 1
    lam, mu = coefs[1, p], coefs[2, p]
    vx, vy, vz = (state[k, p] for k in range(3))
    ax, ay, az = (state[k, p + 1] for k in range(3))
    exx = ax - vx
    eyy = y_after(vy, last) - vy
    ezz = z_after(vz) - vz
    bulk = lam * (exx + eyy + ezz)
    mu2 = mu + mu
    state[3, p] += bulk + mu2 * exx
    state[4, p] += bulk + mu2 * eyy
    state[5, p] += bulk + mu2 * ezz
    state[6, p] += mu * ((z_after(vy) - vy) + (y_after(vz, last) - vz))
    state[7, p] += mu * ((z_after(vx) - vx) + (az - vz))
    state[8, p] += mu * ((y_after(vx, last) - vx) + (ay - vy))


def kernel(
    n_sec, n_depth, fields, block_ids, buoyancy, lame_lambda, lame_mu, moments, owners, cells, rows, out,
    state_a, state_b, leave_a, leave_b, ids, counts, coefs, incs, owner_v, cells_v, rows_v, mom_v, bucket, arrived, lhs, rhs,
    local_sem, raw_send, raw_recv, ids_send, ids_recv, count_send, count_recv, all_send, all_recv,
    first_send, first_recv, second_send, second_recv, inc_send, inc_recv,
):
    sec, depth, seg = lax.axis_index("sec"), lax.axis_index("depth"), lax.axis_index("segment")
    regional, basin = seg == 0, seg == 1

    state_a[...] = jnp.zeros_like(state_a)
    state_b[...] = jnp.zeros_like(state_b)
    ids[...] = jnp.full_like(ids, -1)
    counts[...] = jnp.zeros_like(counts)
    if n_sec < BUCKETS:
        arrived[...] = jnp.zeros_like(arrived)

    barrier = pltpu.get_barrier_semaphore()
    pl.semaphore_signal(barrier, inc=1, device_id=(sec, depth, 1 - seg), device_id_type=MESH)
    expected = jnp.int32(1)
    for dx, dz in NEAR:
        near = in_range(sec + dx, depth + dz, n_sec, n_depth)
        if dz == 0:
            near = jnp.logical_and(near, basin)
        expected = expected + near.astype(I32)

        @pl.when(near)
        def _():
            pl.semaphore_signal(barrier, inc=1, device_id=(sec + dx, depth + dz, seg), device_id_type=MESH)

    @pl.when(regional)
    def _():
        @pl.loop(1, n_sec)
        def _(j):
            pl.semaphore_signal(barrier, inc=1, device_id=(lax.rem(sec + j, n_sec), depth, seg), device_id_type=MESH)

    def load(k, src, dst):
        return pltpu.make_async_copy(src, dst, local_sem.at[k])

    own_state = load(0, fields.at[0], state_a.at[:, OWN_X, OWN_Z])
    own_ids = load(1, block_ids.at[0], ids.at[OWN_X, OWN_Z])
    own_state.start()
    own_ids.start()
    sorting = [load(2, owners, owner_v), load(3, cells, cells_v), load(4, moments, mom_v)]
    counting = load(2, rows, rows_v)

    @pl.when(regional)
    def _():
        for copy in sorting:
            copy.start()
        for copy in sorting:
            copy.wait()
        fill_buckets(owner_v, cells_v, mom_v, bucket, lhs, rhs)
        arrived[sec] = bucket[(sec % 2) * 16 + sec // 2]

    @pl.when(basin)
    def _():
        counting.start()
        counting.wait()
        count_rows(rows_v, counts, lhs, rhs)

    pl.semaphore_wait(barrier, expected + jnp.where(regional, n_sec - 1, 0))

    def passed(j):
        to = lax.rem(sec + j, n_sec)
        return pltpu.make_async_remote_copy(
            src_ref=bucket.at[(to % 2) * 16 + to // 2], dst_ref=arrived.at[sec],
            send_sem=all_send.at[j], recv_sem=all_recv.at[j], device_id=(to, depth, seg), device_id_type=MESH,
        )

    @pl.when(regional)
    def _():
        @pl.loop(0, n_sec - 1)
        def _(t):
            passed(1 + lax.rem(t + n_sec // 2 - 1, n_sec - 1)).start()

    class Exchange:
        def __init__(self, cond, send, recv, source, target):
            self.copies = []
            for q, (dx, dz) in enumerate(NEAR):
                start, size = source_z(dz)
                to = (sec + dx, depth + dz, seg)
                copy = pltpu.make_async_remote_copy(
                    src_ref=source(start, size),
                    dst_ref=target(slice(target_x(dx), target_x(dx) + CX), slice(target_z(dz), target_z(dz) + size)),
                    send_sem=send.at[q], recv_sem=recv.at[q], device_id=to, device_id_type=MESH,
                )
                sends = in_range(sec + dx, depth + dz, n_sec, n_depth)
                gets = in_range(sec - dx, depth - dz, n_sec, n_depth)
                if cond is not None:
                    sends, gets = jnp.logical_and(sends, cond), jnp.logical_and(gets, cond)
                self.copies.append((copy, sends, gets))

        def start(self):
            for copy, sends, _ in self.copies:
                pl.when(sends)(copy.start)

        def wait_recv(self):
            for copy, _, gets in self.copies:
                pl.when(gets)(copy.wait_recv)

        def wait_send(self):
            for copy, sends, _ in self.copies:
                pl.when(sends)(copy.wait_send)

    def own_z(start, size):
        return slice(Z0 + start, Z0 + start + size)

    def cut(start, size):
        return slice(start, start + size)

    raw_all = Exchange(
        basin, raw_send, raw_recv, lambda s, n: fields.at[0, :, :, s:s + n], lambda x, z: state_a.at[:, x, z]
    )
    raw_v = Exchange(
        regional, raw_send, raw_recv, lambda s, n: fields.at[0, 0:3, :, s:s + n], lambda x, z: state_a.at[0:3, x, z]
    )
    raw_ids = Exchange(
        None, ids_send, ids_recv, lambda s, n: block_ids.at[0, :, s:s + n], lambda x, z: ids.at[x, z]
    )
    raw_counts = Exchange(
        basin, count_send, count_recv, lambda s, n: counts.at[OWN_X, own_z(s, n)], lambda x, z: counts.at[x, z]
    )
    first = Exchange(
        regional, first_send, first_recv,
        lambda s, n: leave_a.at[3:9, :, cut(s, n)], lambda x, z: state_a.at[3:9, x, z],
    )
    second = Exchange(
        None, second_send, second_recv,
        lambda s, n: leave_b.at[:, :, cut(s, n)], lambda x, z: state_b.at[:, x, z],
    )
    raw_ids.start()
    raw_v.start()
    raw_all.start()
    raw_counts.start()

    own_ids.wait()
    raw_ids.wait_recv()
    look_up(ids, (buoyancy, lame_lambda, lame_mu), coefs)
    own_state.wait()

    @pl.when(regional)
    def _():
        @pl.loop(1, n_sec)
        def _(j):
            come = lax.rem(sec + n_sec - j, n_sec)
            pltpu.make_async_remote_copy(
                src_ref=bucket.at[0], dst_ref=arrived.at[come], send_sem=all_send.at[j], recv_sem=all_recv.at[j],
                device_id=(come, depth, seg), device_id_type=MESH,
            ).wait_recv()

        add_buckets(arrived, state_a, leave_a, lhs, rhs)

    first.start()
    raw_v.wait_recv()
    raw_all.wait_recv()
    raw_counts.wait_recv()
    first.wait_recv()

    def coupled(step, p):
        return pltpu.make_async_remote_copy(
            src_ref=incs.at[step, :, p], dst_ref=incs.at[step, :, p], send_sem=inc_send.at[step, p],
            recv_sem=inc_recv.at[step, p], device_id=(sec, depth, 1), device_id_type=MESH,
        )

    def advance(state, step, planes):
        @pl.when(regional)
        def _():
            for p in planes:
                for k, inc in enumerate(increments(state, coefs, p)):
                    incs[step, k, p] = inc
                    state[k, p] += inc
                coupled(step, p).start()

        @pl.when(basin)
        def _():
            for p in planes:
                mine = increments(state, coefs, p)
                coupled(step, p).wait_recv()
                count = counts[p]
                for k, inc in enumerate(mine):
                    state[k, p] += inc + count * incs[step, k, p]

        for p in planes[:-1]:
            stress(state, coefs, p)

    wide, narrow = range(X0 - 1, X0 + CX + 2), range(X0, X0 + CX + 1)
    advance(state_a, 0, wide)
    advance(state_a, 1, narrow)
    half_way = state_a[:, OWN_X, OWN_Z]
    leave_b[...] = half_way
    state_b[:, OWN_X, OWN_Z] = half_way
    second.start()
    second.wait_recv()
    advance(state_b, 2, wide)
    advance(state_b, 3, narrow)

    result = load(5, state_b.at[:, OWN_X, OWN_Z], out.at[0])
    result.start()

    raw_ids.wait_send()
    raw_v.wait_send()
    raw_all.wait_send()
    raw_counts.wait_send()
    first.wait_send()
    second.wait_send()

    @pl.when(regional)
    def _():
        @pl.loop(1, n_sec)
        def _(j):
            passed(j).wait_send()

        for step in range(4):
            for p in (wide, narrow)[step % 2]:
                coupled(step, p).wait_send()

    result.wait()


def on_device(
    n_sec, n_depth, fields, block_ids, buoyancy, lame_lambda, lame_mu, moments, moment_owner, moment_cells, drm_rows
):
    owners = moment_owner.reshape(ENT // 128, 128)
    cells = moment_cells.reshape(ENT // 128, 128)
    rows = drm_rows.reshape(ROWS // 128, 128)
    hbm = pl.BlockSpec(memory_space=pl.ANY)
    smem = pl.BlockSpec(memory_space=pltpu.SMEM)
    dma = pltpu.SemaphoreType.DMA
    near = [dma((len(NEAR),))] * 2
    block = (9, PX, RZ, CY)
    return pl.pallas_call(
        functools.partial(kernel, n_sec, n_depth),
        out_shape=jax.ShapeDtypeStruct(fields.shape, F32),
        in_specs=[hbm, hbm, smem, smem, smem, hbm, hbm, hbm, hbm],
        out_specs=hbm,
        scratch_shapes=[
            pltpu.VMEM(block, F32),
            pltpu.VMEM(block, F32),
            pltpu.VMEM((9, CX, CZ, CY), F32),
            pltpu.VMEM((9, CX, CZ, CY), F32),
            pltpu.VMEM(block[1:], I32),
            pltpu.VMEM(block[1:], F32),
            pltpu.VMEM((3,) + block[1:], F32),
            pltpu.VMEM((4, 3) + block[1:], F32),
            pltpu.VMEM((ENT // 128, 128), I32),
            pltpu.VMEM((ENT // 128, 128), I32),
            pltpu.VMEM((ROWS // 128, 128), I32),
            pltpu.VMEM((6, ENT), F32),
            pltpu.VMEM((BUCKETS, 4, 128), F32),
            pltpu.VMEM((BUCKETS, 4, 128), F32),
            pltpu.VMEM((192, 2048), BF16),
            pltpu.VMEM((256, 2048), BF16),
            dma((6,)),
            *near, *near, *near,
            dma((BUCKETS,)), dma((BUCKETS,)),
            *near, *near,
            dma((4, PX)), dma((4, PX)),
        ],
        compiler_params=pltpu.CompilerParams(collective_id=0, has_side_effects=True),
    )(fields, block_ids, buoyancy, lame_lambda, lame_mu, moments, owners, cells, rows)


def solution(mesh):
    in_specs = (
        P("segment", None, "sec", "depth", None),
        P("segment", "sec", "depth", None),
        P(),
        P(),
        P(),
        P(None, ("sec", "depth")),
        P(("sec", "depth"), None),
        P(("sec", "depth")),
        P(("sec", "depth")),
    )
    return jax.shard_map(
        functools.partial(on_device, mesh.shape["sec"], mesh.shape["depth"]),
        mesh=mesh, in_specs=in_specs, out_specs=P("segment", None, "sec", "depth", None), check_vma=False,
    )
```

time: 606 us -> 35.9 us (0.06)
  other arithmetic: 270 us -> 0 us
  local copies, waits for them, and re-layouts: 111 us -> 1.58 us
  blocking collectives: 105 us -> 0 us
  waiting for transfers between devices: 67.7 us -> 0 us
  starting transfers between devices: 45 us -> 0 us
  Pallas kernels: 0 us -> 34.1 us
    scatter-add x5 -> x0, other arithmetic: 224 us -> none  [the longest x1 175 us: on_device(): stress = fields[0, 3:].reshape(6, -1).at[:, places].add(values, mode='drop')]
    all_gather x3 -> x0, blocking collectives: 105 us -> none  [the longest x1 41.3 us: on_device(): lax.all_gather(moments, 'sec', axis=1, tiled=True)]
    ppermute x20 -> x0, waiting for transfers between devices: 67.7 us -> none  [passed_along(): return lax.ppermute(block, axis, route)]
    ppermute x20 -> x0, starting transfers between devices: 45 us -> none  [passed_along(): return lax.ppermute(block, axis, route)]
    unnamed x57 -> x1, local copies, waits for them, and re-layouts: 36 us -> 1.58 us
    pallas_call x0 -> x1, Pallas kernels: none -> 34.1 us  [on_device(): pl.pallas_call(functools.partial(kernel, n_sec, n_depth), out_shape=jax.S...]
    add x15 -> x0, other arithmetic: 31.9 us -> none  [the longest x3 20.5 us: advance(): syy = syy + HALF_STEP * (lam * trace + 2.0 * shear * eyy)]
    gather x8 -> x0, local copies, waits for them, and re-layouts: 30 us -> none  [couple(): increment = (newv[0] - oldv[0]).reshape(3, -1)[:, rows_here]]
  transfers between devices with their start and end apart: 20 -> 0, of which waited for: 14 -> 0; matrix products, arithmetic and copies ran while one was open for 10% -> 0% of each run, Pallas kernels for 0% -> 0%
where the time goes in v1:
time: 35.9 us; the launch traced here: 35.7 us
  Pallas kernels  34.1 us (95%)
  local copies, waits for them, and re-layouts  1.58 us (4%)
    pallas_call x1, Pallas kernels, on_device(): pl.pallas_call(functools.partial(kernel, n_sec, n_depth), out_shape=jax.S...  34.1 us
    unnamed x1, local copies, waits for them, and re-layouts  1.58 us

profile of v1, /device:TPU:31, one launch (start us, length us, event | category | flops | bytes accessed | tf_op | source)
XLA Modules:
  0.0 35.7 jit_solution(11518831764230211535)
XLA Ops:
  0.0 34.1 %shard_map.91 = f32[1,9,2,16,128]{4,3,2,1,0:T(8,128)} custom-call(f32[1,9,2,16,128]{4,3,2,1,0:T(8,128)} %fields.1, s32[1,2,16,128]{3,2,1,0:T(8,128)} %block_ids.1, f32[16]{0:T(128)} %buoyancy.1, f32[16]{0:T(128)} %lame_lambda.1, f32[16]{0:T(128)} %lame_mu.1, f32[6,1024]{1,0:T(8,128)} %moments.1, s32[8,128]{1,0:T(8,128)} %bitcast.4, s32[8,128]{1,0:T(8,128)} %bitcast.5, ...), custom_call_target="tpu_custom_call" | custom-call | tf_op jit(solution)/shard_map/pallas_call | solution.py:414
  34.1 1.6 %copy.11 = f32[1,9,2,16,128]{4,3,2,1,0:T(8,128)} copy(f32[1,9,2,16,128]{4,3,2,1,0:T(8,128)} %shard_map.91) | data formatting | bytes 294912

commit v2 on v1

v2 whole, which is shorter than its diff:
```python
import functools

import jax
import jax.numpy as jnp
from jax import lax
from jax.experimental import pallas as pl
from jax.experimental.pallas import tpu as pltpu
from jax.sharding import PartitionSpec as P

MESH = pl.DeviceIdType.MESH
CX, CZ, CY = 2, 16, 128
ENT, ROWS, CAP, BUCKETS = 1024, 2048, 64, 32
HZ, RIM = CZ // 2, 4
PX, RZ, GZ = CX + 4, HZ + 2 * RIM, CZ + 2 * RIM
X0 = 2
OWN_X, OWN_Z = slice(X0, X0 + CX), slice(RIM, RIM + HZ)
NEAR = tuple((dx, dz) for dx in (-1, 0, 1) for dz in (-1, 0, 1) if (dx, dz) != (0, 0))
NT = (((1,), (1,)), ((), ()))
BF16, F32, I32 = jnp.bfloat16, jnp.float32, jnp.int32


def split(value):
    high = value.astype(BF16).astype(F32)
    return high, value - high


def rows_at(start, size):
    return slice(start, start + size)


def beside(dx):
    return rows_at(X0 - CX * dx, CX)


def in_range(sec, depth, n_sec, n_depth):
    ok_sec = jnp.logical_and(sec >= 0, sec < n_sec)
    ok_depth = jnp.logical_and(depth >= 0, depth < n_depth)
    return jnp.logical_and(ok_sec, ok_depth)


def fill_buckets(owner, cells, mom, bucket, lhs, rhs):
    owners = [owner[t:t + 1, :] for t in range(8)]
    row32 = lax.broadcasted_iota(I32, (BUCKETS, 128), 0)
    hot = [jnp.where(row32 == o, 1.0, 0.0) for o in owners]
    before = jnp.where(
        lax.broadcasted_iota(I32, (128, 256), 0) < lax.broadcasted_iota(I32, (128, 256), 1), 1.0, 0.0
    ).astype(BF16)
    counts = jnp.dot(jnp.concatenate(hot, 0).astype(BF16), before, preferred_element_type=F32)
    running = jnp.zeros((BUCKETS, 128), F32)
    row16 = lax.broadcasted_iota(I32, (16, 128), 0)
    row256 = lax.broadcasted_iota(I32, (256, 128), 0)
    for t in range(8):
        part = counts[t * BUCKETS:(t + 1) * BUCKETS]
        rank = jnp.sum(hot[t] * (part[:, :128] + running), axis=0, keepdims=True).astype(I32)
        running = running + part[:, 128:]
        cols = slice(t * 128, (t + 1) * 128)
        slot = (owners[t] & 1) * 128 + rank
        mine = row16 == (owners[t] >> 1)
        cell = cells[t:t + 1, :].astype(F32)
        for h in range(2):
            at = slice((2 * t + h) * 128, (2 * t + h + 1) * 128)
            rhs[:, at] = jnp.where(row256 == slot + h * CAP, 1.0, 0.0).astype(BF16)
            for j in range(4):
                value = mom[2 * j + h:2 * j + h + 1, cols] if j < 3 else cell
                high, low = split(value)
                lhs[j * 16:(j + 1) * 16, at] = jnp.where(mine, high, 0.0).astype(BF16)
                lhs[64 + j * 16:64 + (j + 1) * 16, at] = jnp.where(mine, low, 0.0).astype(BF16)
    sums = lax.dot_general(lhs[0:128, :], rhs[...], NT, preferred_element_type=F32)
    sums = sums[0:64] + sums[64:128]
    for j in range(4):
        for x in range(2):
            bucket[x * 16:(x + 1) * 16, j, :] = sums[j * 16:(j + 1) * 16, x * 128:(x + 1) * 128]


def place(cell):
    return (cell >> 7) & 15, ((cell >> 11) << 7) | (cell & 127)


def add_buckets(arrived, raw, leaving, lhs, rhs):
    low_half = lax.broadcasted_iota(I32, (16, 128), 1) < CAP
    values, cell = [], None
    for j in range(4):
        rows = arrived[:, j, :]
        a, b = rows[0:16], rows[16:32]
        even = jnp.where(low_half, a, pltpu.roll(b, CAP, 1))
        if j < 3:
            values.append(even)
            values.append(jnp.where(low_half, pltpu.roll(a, CAP, 1), b))
        else:
            cell = even.astype(I32)
    z, lane = place(cell)
    parts = [split(value) for value in values]
    row16 = lax.broadcasted_iota(I32, (16, 128), 0)
    row256 = lax.broadcasted_iota(I32, (256, 128), 0)
    for t in range(16):
        at = slice(t * 128, (t + 1) * 128)
        mine = row16 == z[t:t + 1]
        rhs[:, at] = jnp.where(row256 == lane[t:t + 1], 1.0, 0.0).astype(BF16)
        for k, (high, low) in enumerate(parts):
            lhs[k * 16:(k + 1) * 16, at] = jnp.where(mine, high[t:t + 1], 0.0).astype(BF16)
            lhs[96 + k * 16:96 + (k + 1) * 16, at] = jnp.where(mine, low[t:t + 1], 0.0).astype(BF16)
    sums = lax.dot_general(lhs[...], rhs[...], NT, preferred_element_type=F32)
    sums = sums[0:96] + sums[96:192]
    for k in range(6):
        for x in range(CX):
            leaving[k, x] = raw[k, x] + sums[k * 16:(k + 1) * 16, x * 128:(x + 1) * 128]


def count_rows(rows, counted, lhs, rhs):
    z, lane = place(rows[...])
    row16 = lax.broadcasted_iota(I32, (16, 128), 0)
    row256 = lax.broadcasted_iota(I32, (256, 128), 0)
    for t in range(16):
        at = slice(t * 128, (t + 1) * 128)
        lhs[0:16, at] = jnp.where(row16 == z[t:t + 1], 1.0, 0.0).astype(BF16)
        rhs[:, at] = jnp.where(row256 == lane[t:t + 1], 1.0, 0.0).astype(BF16)
    sums = lax.dot_general(lhs[0:16, :], rhs[...], NT, preferred_element_type=F32)
    for x in range(CX):
        counted[x] = sums[:, x * 128:(x + 1) * 128]


def place(cell):
    return (cell >> 7) & 15, ((cell >> 11) << 7) | (cell & 127)


def look_up(ids, tables, coefs):
    for m in range(2):
        for p in range(PX):
            block = ids[m, p]
            values = [jnp.zeros((RZ, CY), F32) for _ in tables]
            for entry in range(16):
                here = block == entry
                values = [jnp.where(here, table[entry], v) for table, v in zip(tables, values)]
            for k, v in enumerate(values):
                coefs[m, k, p] = 0.5 * v


def y_before(f, first):
    return jnp.where(first, 0.0, pltpu.roll(f, 1, 1))


def y_after(f, last):
    return jnp.where(last, 0.0, pltpu.roll(f, CY - 1, 1))


def z_before(f):
    return pltpu.roll(f, 1, 0)


def z_after(f):
    return pltpu.roll(f, RZ - 1, 0)


def increments(state, coefs, m, p):
    first = lax.broadcasted_iota(I32, (RZ, CY), 1) == 0
    b = coefs[m, 0, p]
    sxx, syy, szz, syz, sxz, sxy = (state[m, k, p] for k in range(3, 9))
    bxx, bxz, bxy = (state[m, k, p - 1] for k in (3, 7, 8))
    ix = b * ((sxx - bxx) + (sxy - y_before(sxy, first)) + (sxz - z_before(sxz)))
    iy = b * ((sxy - bxy) + (syy - y_before(syy, first)) + (syz - z_before(syz)))
    iz = b * ((sxz - bxz) + (syz - y_before(syz, first)) + (szz - z_before(szz)))
    return ix, iy, iz


def velocity(state, coefs, counts, planes):
    for p in planes:
        count = counts[p]
        regional, basin = increments(state, coefs, 0, p), increments(state, coefs, 1, p)
        for k in range(3):
            state[0, k, p] += regional[k]
            state[1, k, p] += basin[k] + count * regional[k]


def stress(state, coefs, planes):
    last = lax.broadcasted_iota(I32, (RZ, CY), 1) == CY - 1
    for m in range(2):
        for p in planes:
            lam, mu = coefs[m, 1, p], coefs[m, 2, p]
            vx, vy, vz = (state[m, k, p] for k in range(3))
            ax, ay, az = (state[m, k, p + 1] for k in range(3))
            exx = ax - vx
            eyy = y_after(vy, last) - vy
            ezz = z_after(vz) - vz
            bulk = lam * (exx + eyy + ezz)
            mu2 = mu + mu
            state[m, 3, p] += bulk + mu2 * exx
            state[m, 4, p] += bulk + mu2 * eyy
            state[m, 5, p] += bulk + mu2 * ezz
            state[m, 6, p] += mu * ((z_after(vy) - vy) + (y_after(vz, last) - vz))
            state[m, 7, p] += mu * ((z_after(vx) - vx) + (az - vz))
            state[m, 8, p] += mu * ((y_after(vx, last) - vx) + (ay - vy))


class Group:
    def __init__(self):
        self.copies = []

    def add(self, copy, sends, gets):
        self.copies.append((copy, sends, gets))

    def start(self):
        for copy, sends, _ in self.copies:
            pl.when(sends)(copy.start)

    def wait_recv(self):
        for copy, _, gets in self.copies:
            pl.when(gets)(copy.wait_recv)

    def wait_send(self):
        for copy, sends, _ in self.copies:
            pl.when(sends)(copy.wait_send)


def kernel(
    n_sec, n_depth, fields, block_ids, buoyancy, lame_lambda, lame_mu, moments, owners, cells, rows, out,
    staged, staged_ids, state, ids, counts, coefs, raw_stress, leaving, counted, to_right, to_left, from_left, from_right,
    owner_v, cells_v, rows_v, mom_v, bucket, arrived, lhs, rhs,
    local_sem, core_send, core_recv, raw_send, raw_recv, ids_send, ids_recv, count_send, count_recv, all_send, all_recv,
    first_send, first_recv, second_send, second_recv,
):
    sec, depth, seg = lax.axis_index("sec"), lax.axis_index("depth"), lax.axis_index("segment")
    partner = (sec, depth, 1 - seg)

    def load(k, src, dst):
        return pltpu.make_async_copy(src, dst, local_sem.at[k])

    def remote(src, dst, send, recv, to):
        return pltpu.make_async_remote_copy(
            src_ref=src, dst_ref=dst, send_sem=send, recv_sem=recv, device_id=to, device_id_type=MESH
        )

    def there(dx, dz):
        return in_range(sec + dx, depth + dz, n_sec, n_depth)

    loads = [load(0, owners, owner_v), load(1, cells, cells_v), load(2, moments, mom_v), load(3, rows, rows_v)]
    for copy in loads:
        copy.start()

    staged[...] = jnp.zeros_like(staged)
    staged_ids[...] = jnp.full_like(staged_ids, -1)
    state[0, 3:9] = jnp.zeros_like(state[0, 3:9])
    counts[...] = jnp.zeros_like(counts)
    if n_sec < BUCKETS:
        arrived[...] = jnp.zeros_like(arrived)

    barrier = pltpu.get_barrier_semaphore()
    expected = jnp.int32(n_sec)

    @pl.loop(1, n_sec)
    def _(j):
        pl.semaphore_signal(barrier, inc=1, device_id=(lax.rem(sec + j, n_sec), depth, seg), device_id_type=MESH)

    pl.semaphore_signal(barrier, inc=1, device_id=partner, device_id_type=MESH)
    for dx, dz in NEAR:
        if dz != 0:
            near = there(dx, dz)
            expected = expected + near.astype(I32)

            @pl.when(near)
            def _():
                pl.semaphore_signal(barrier, inc=1, device_id=(sec + dx, depth + dz, seg), device_id_type=MESH)

    own_state = load(4, fields.at[0], staged.at[:, OWN_X, rows_at(RIM, CZ)])
    own_ids = load(5, block_ids.at[0], staged_ids.at[OWN_X, rows_at(RIM, CZ)])
    own_stress = load(6, fields.at[0, 3:9], raw_stress)
    own_state.start()
    own_ids.start()
    pl.when(seg == 0)(own_stress.start)

    for copy in loads:
        copy.wait()
    fill_buckets(owner_v, cells_v, mom_v, bucket, lhs, rhs)

    pl.semaphore_wait(barrier, expected)

    def passed(j):
        to = lax.rem(sec + j, n_sec)
        return remote(
            bucket.at[lax.rem(to, 2) * 16 + to // 2], arrived.at[sec], all_send.at[j], all_recv.at[j], (to, depth, seg)
        )

    @pl.loop(0, n_sec - 1)
    def _(t):
        passed(1 + lax.rem(t + n_sec // 2 - 1, n_sec - 1)).start()

    arrived[sec] = bucket[lax.rem(sec, 2) * 16 + sec // 2]

    raw, raw_ids = Group(), Group()
    for q, (dx, dz) in enumerate(NEAR):
        from_z = {-1: rows_at(0, RIM), 0: rows_at(0, CZ), 1: rows_at(CZ - RIM, RIM)}[dz]
        to_z = {-1: rows_at(RIM + CZ, RIM), 0: rows_at(RIM, CZ), 1: rows_at(0, RIM)}[dz]
        to = (sec + dx, depth + dz, seg)
        sends, gets = there(dx, dz), there(-dx, -dz)
        for m, parts in ((0, slice(0, 3)), (1, slice(0, 9))):
            raw.add(
                remote(fields.at[0, parts, :, from_z], staged.at[parts, beside(dx), to_z], raw_send.at[q], raw_recv.at[q], to),
                jnp.logical_and(sends, seg == m), jnp.logical_and(gets, seg == m),
            )
        raw_ids.add(
            remote(block_ids.at[0, :, from_z], staged_ids.at[beside(dx), to_z], ids_send.at[q], ids_recv.at[q], to),
            sends, gets,
        )
    partner_stress = remote(fields.at[0, 3:9], raw_stress, core_send.at[0], core_recv.at[0], partner)
    raw_ids.start()
    pl.when(seg == 0)(partner_stress.start)
    raw.start()

    def window(source, target, send, recv):
        group = Group()
        for c in range(2):
            dz = 1 - 2 * c
            for q, (dx, goes) in enumerate(((-1, 0), (1, 0), (0, dz), (-1, dz), (1, dz))):
                if goes == 0:
                    from_z, to_z = rows_at(RIM * c, HZ + RIM), rows_at(RIM * (1 - c), HZ + RIM)
                else:
                    from_z, to_z = rows_at((CZ - RIM) * (1 - c), RIM), rows_at((HZ + RIM) * c, RIM)
                group.add(
                    remote(source(from_z), target(beside(dx), to_z), send.at[q], recv.at[q], (sec + dx, depth + goes, seg)),
                    jnp.logical_and(there(dx, goes), seg == c), jnp.logical_and(there(-dx, -goes), seg == c),
                )
        return group

    count_rows(rows_v, counted, lhs, rhs)
    for c in range(2):
        @pl.when(seg == c)
        def _():
            counts[OWN_X, rows_at(RIM * (1 - c), HZ + RIM)] = counted[:, rows_at(RIM * c, HZ + RIM)]

    near_counts = window(lambda z: counted.at[:, z], lambda x, z: counts.at[x, z], count_send, count_recv)
    near_counts.start()

    own_ids.wait()
    raw_ids.wait_recv()
    hand_ids, keep_ids, hand, keep = [], [], [], []
    for m, parts in ((0, slice(0, 3)), (1, slice(0, 9))):
        mine, theirs = rows_at(HZ * m, RZ), rows_at(HZ * (1 - m), RZ)
        hand_ids.append(remote(staged_ids.at[:, theirs], ids.at[m], core_send.at[1], core_recv.at[1], partner))
        keep_ids.append(load(7, staged_ids.at[:, mine], ids.at[m]))
        hand.append(remote(staged.at[parts, :, theirs], state.at[m, parts], core_send.at[2], core_recv.at[2], partner))
        keep.append(load(8, staged.at[parts, :, mine], state.at[m, parts]))

        @pl.when(seg == m)
        def _():
            hand_ids[m].start()
            keep_ids[m].start()

    own_state.wait()
    raw.wait_recv()
    for m in range(2):
        @pl.when(seg == m)
        def _():
            hand[m].start()
            keep[m].start()
    for m in range(2):
        @pl.when(seg == m)
        def _():
            keep_ids[m].wait()
            hand_ids[1 - m].wait_recv()
    look_up(ids, (buoyancy, lame_lambda, lame_mu), coefs)
    pl.when(seg == 0)(own_stress.wait)
    pl.when(seg == 1)(partner_stress.wait_recv)

    @pl.loop(1, n_sec)
    def _(j):
        come = lax.rem(sec + n_sec - j, n_sec)
        remote(bucket.at[0], arrived.at[come], all_send.at[j], all_recv.at[j], (come, depth, seg)).wait_recv()

    add_buckets(arrived, raw_stress, leaving, lhs, rhs)
    first = window(lambda z: leaving.at[:, :, z], lambda x, z: state.at[0, 3:9, x, z], first_send, first_recv)
    first.start()
    for c in range(2):
        @pl.when(seg == c)
        def _():
            state[0, 3:9, OWN_X, rows_at(RIM * (1 - c), HZ + RIM)] = leaving[:, :, rows_at(RIM * c, HZ + RIM)]

    for m in range(2):
        @pl.when(seg == m)
        def _():
            keep[m].wait()
            hand[1 - m].wait_recv()
    near_counts.wait_recv()
    first.wait_recv()

    lo, hi = X0, X0 + CX - 1
    velocity(state, coefs, counts, range(lo - 1, hi + 3))
    stress(state, coefs, range(lo - 1, hi + 2))
    velocity(state, coefs, counts, range(lo, hi + 2))
    stress(state, coefs, range(lo, hi + 1))
    velocity(state, coefs, counts, (hi,))
    for m in range(2):
        for k in range(3):
            to_right[m, k] = state[m, k, hi]
            to_left[m, k] = state[m, k, hi]
        for k, part in enumerate((3, 7, 8)):
            to_right[m, 3 + k] = state[m, part, hi]
        for k in range(3, 9):
            to_left[m, k] = state[m, k, lo]

    second = Group()
    z = rows_at(2, RZ - 4)
    for q, (dx, src, dst) in enumerate(((1, to_right, from_left), (-1, to_left, from_right))):
        second.add(
            remote(src.at[:, :, z], dst.at[:, :, z], second_send.at[q], second_recv.at[q], (sec + dx, depth, seg)),
            there(dx, 0), there(-dx, 0),
        )
    second.start()
    second.wait_recv()

    @pl.when(there(-1, 0))
    def _():
        for m in range(2):
            for k, part in enumerate((0, 1, 2, 3, 7, 8)):
                state[m, part, lo - 1] = from_left[m, k]

    @pl.when(there(1, 0))
    def _():
        for m in range(2):
            for k in range(3):
                state[m, k, hi + 2] = from_right[m, k]
            for k in range(3, 9):
                state[m, k, hi + 1] = from_right[m, k]

    velocity(state, coefs, counts, (lo, hi + 1))
    stress(state, coefs, range(lo - 1, hi + 2))
    velocity(state, coefs, counts, range(lo, hi + 2))
    stress(state, coefs, range(lo, hi + 1))

    results = []
    for c in range(2):
        part = rows_at(HZ * c, HZ)
        keeps = load(9, state.at[c, :, OWN_X, OWN_Z], out.at[0, :, :, part])
        gives = remote(state.at[1 - c, :, OWN_X, OWN_Z], out.at[0, :, :, part], core_send.at[3], core_recv.at[3], partner)
        results.append((keeps, gives))

        @pl.when(seg == c)
        def _():
            gives.start()
            keeps.start()

    for group in (raw, raw_ids, near_counts, first, second):
        group.wait_send()
    pl.when(seg == 0)(partner_stress.wait_send)
    for c in range(2):
        @pl.when(seg == c)
        def _():
            hand_ids[c].wait_send()
            hand[c].wait_send()

    @pl.loop(1, n_sec)
    def _(j):
        passed(j).wait_send()

    for c in range(2):
        @pl.when(seg == c)
        def _():
            results[c][0].wait()
            results[c][1].wait_send()
            results[1 - c][1].wait_recv()


def on_device(
    n_sec, n_depth, fields, block_ids, buoyancy, lame_lambda, lame_mu, moments, moment_owner, moment_cells, drm_rows
):
    owners = moment_owner.reshape(ENT // 128, 128)
    cells = moment_cells.reshape(ENT // 128, 128)
    rows = drm_rows.reshape(ROWS // 128, 128)
    hbm = pl.BlockSpec(memory_space=pl.ANY)
    smem = pl.BlockSpec(memory_space=pltpu.SMEM)
    dma = pltpu.SemaphoreType.DMA
    vmem = pltpu.VMEM
    return pl.pallas_call(
        functools.partial(kernel, n_sec, n_depth),
        out_shape=jax.ShapeDtypeStruct(fields.shape, F32),
        in_specs=[hbm, hbm, smem, smem, smem, hbm, hbm, hbm, hbm],
        out_specs=hbm,
        scratch_shapes=[
            vmem((9, PX, GZ, CY), F32),
            vmem((PX, GZ, CY), I32),
            vmem((2, 9, PX, RZ, CY), F32),
            vmem((2, PX, RZ, CY), I32),
            vmem((PX, RZ, CY), F32),
            vmem((2, 3, PX, RZ, CY), F32),
            vmem((6, CX, CZ, CY), F32),
            vmem((6, CX, CZ, CY), F32),
            vmem((CX, CZ, CY), F32),
            vmem((2, 6, RZ, CY), F32),
            vmem((2, 9, RZ, CY), F32),
            vmem((2, 6, RZ, CY), F32),
            vmem((2, 9, RZ, CY), F32),
            vmem((ENT // 128, 128), I32),
            vmem((ENT // 128, 128), I32),
            vmem((ROWS // 128, 128), I32),
            vmem((6, ENT), F32),
            vmem((BUCKETS, 4, 128), F32),
            vmem((BUCKETS, 4, 128), F32),
            vmem((192, 2048), BF16),
            vmem((256, 2048), BF16),
            dma((10,)),
            dma((4,)), dma((4,)),
            dma((8,)), dma((8,)),
            dma((8,)), dma((8,)),
            dma((5,)), dma((5,)),
            dma((BUCKETS,)), dma((BUCKETS,)),
            dma((5,)), dma((5,)),
            dma((2,)), dma((2,)),
        ],
        compiler_params=pltpu.CompilerParams(collective_id=0, has_side_effects=True),
    )(fields, block_ids, buoyancy, lame_lambda, lame_mu, moments, owners, cells, rows)


def solution(mesh):
    in_specs = (
        P("segment", None, "sec", "depth", None),
        P("segment", "sec", "depth", None),
        P(),
        P(),
        P(),
        P(None, ("sec", "depth")),
        P(("sec", "depth"), None),
        P(("sec", "depth")),
        P(("sec", "depth")),
    )
    return jax.shard_map(
        functools.partial(on_device, mesh.shape["sec"], mesh.shape["depth"]),
        mesh=mesh, in_specs=in_specs, out_specs=P("segment", None, "sec", "depth", None), check_vma=False,
    )
```

time: 35.9 us -> 34.4 us (0.958); the launches traced: 35.7 us -> 33.7 us
  Pallas kernels: 34.1 us -> 32.1 us
    pallas_call x1, Pallas kernels: 34.1 us -> 32.1 us  [on_device(): pl.pallas_call(functools.partial(kernel, n_sec, n_depth), out_shape=jax.S...]
where the time goes in v2:
time: 34.4 us; the launch traced here: 33.7 us
  Pallas kernels  32.1 us (93%)
  local copies, waits for them, and re-layouts  1.58 us (5%)
    pallas_call x1, Pallas kernels, on_device(): pl.pallas_call(functools.partial(kernel, n_sec, n_depth), out_shape=jax.S...  32.1 us
    unnamed x1, local copies, waits for them, and re-layouts  1.58 us

profile of v2, /device:TPU:31, one launch (start us, length us, event | category | flops | bytes accessed | tf_op | source)
XLA Modules:
  0.0 33.7 jit_solution(16258705649133655268)
XLA Ops:
  0.0 32.1 %shard_map.91 = f32[1,9,2,16,128]{4,3,2,1,0:T(8,128)} custom-call(f32[1,9,2,16,128]{4,3,2,1,0:T(8,128)} %fields.1, s32[1,2,16,128]{3,2,1,0:T(8,128)} %block_ids.1, f32[16]{0:T(128)} %buoyancy.1, f32[16]{0:T(128)} %lame_lambda.1, f32[16]{0:T(128)} %lame_mu.1, f32[6,1024]{1,0:T(8,128)} %moments.1, s32[8,128]{1,0:T(8,128)} %bitcast.4, s32[8,128]{1,0:T(8,128)} %bitcast.5, ...), custom_call_target="tpu_custom_call" | custom-call | tf_op jit(solution)/shard_map/pallas_call | solution.py:471
  32.2 1.6 %copy.11 = f32[1,9,2,16,128]{4,3,2,1,0:T(8,128)} copy(f32[1,9,2,16,128]{4,3,2,1,0:T(8,128)} %shard_map.91) | data formatting | bytes 294912

commit v3 on v2

--- a/solution.py
+++ b/solution.py
@@ -127,10 +127,10 @@
     for m in range(2):
         for p in range(PX):
             block = ids[m, p]
-            values = [jnp.zeros((RZ, CY), F32) for _ in tables]
+            values = [jnp.zeros((RZ, CY), F32) for _ in range(3)]
             for entry in range(16):
                 here = block == entry
-                values = [jnp.where(here, table[entry], v) for table, v in zip(tables, values)]
+                values = [jnp.where(here, tables[k, entry], v) for k, v in enumerate(values)]
             for k, v in enumerate(values):
                 coefs[m, k, p] = 0.5 * v
 
@@ -213,7 +213,7 @@
 
 def kernel(
     n_sec, n_depth, fields, block_ids, buoyancy, lame_lambda, lame_mu, moments, owners, cells, rows, out,
-    staged, staged_ids, state, ids, counts, coefs, raw_stress, leaving, counted, to_right, to_left, from_left, from_right,
+    tables, staged, staged_ids, state, ids, counts, coefs, raw_stress, leaving, counted, to_right, to_left, from_left, from_right,
     owner_v, cells_v, rows_v, mom_v, bucket, arrived, lhs, rhs,
     local_sem, core_send, core_recv, raw_send, raw_recv, ids_send, ids_recv, count_send, count_recv, all_send, all_recv,
     first_send, first_recv, second_send, second_recv,
@@ -233,7 +233,8 @@
         return in_range(sec + dx, depth + dz, n_sec, n_depth)
 
     loads = [load(0, owners, owner_v), load(1, cells, cells_v), load(2, moments, mom_v), load(3, rows, rows_v)]
-    for copy in loads:
+    table_loads = [load(10 + k, table, tables.at[k]) for k, table in enumerate((buoyancy, lame_lambda, lame_mu))]
+    for copy in loads + table_loads:
         copy.start()
 
     staged[...] = jnp.zeros_like(staged)
@@ -329,6 +330,22 @@
     near_counts = window(lambda z: counted.at[:, z], lambda x, z: counts.at[x, z], count_send, count_recv)
     near_counts.start()
 
+    pl.when(seg == 0)(own_stress.wait)
+    pl.when(seg == 1)(partner_stress.wait_recv)
+
+    @pl.loop(1, n_sec)
+    def _(j):
+        come = lax.rem(sec + n_sec - j, n_sec)
+        remote(bucket.at[0], arrived.at[come], all_send.at[j], all_recv.at[j], (come, depth, seg)).wait_recv()
+
+    add_buckets(arrived, raw_stress, leaving, lhs, rhs)
+    first = window(lambda z: leaving.at[:, :, z], lambda x, z: state.at[0, 3:9, x, z], first_send, first_recv)
+    first.start()
+    for c in range(2):
+        @pl.when(seg == c)
+        def _():
+            state[0, 3:9, OWN_X, rows_at(RIM * (1 - c), HZ + RIM)] = leaving[:, :, rows_at(RIM * c, HZ + RIM)]
+
     own_ids.wait()
     raw_ids.wait_recv()
     hand_ids, keep_ids, hand, keep = [], [], [], []
@@ -356,23 +373,9 @@
         def _():
             keep_ids[m].wait()
             hand_ids[1 - m].wait_recv()
-    look_up(ids, (buoyancy, lame_lambda, lame_mu), coefs)
-    pl.when(seg == 0)(own_stress.wait)
-    pl.when(seg == 1)(partner_stress.wait_recv)
-
-    @pl.loop(1, n_sec)
-    def _(j):
-        come = lax.rem(sec + n_sec - j, n_sec)
-        remote(bucket.at[0], arrived.at[come], all_send.at[j], all_recv.at[j], (come, depth, seg)).wait_recv()
-
-    add_buckets(arrived, raw_stress, leaving, lhs, rhs)
-    first = window(lambda z: leaving.at[:, :, z], lambda x, z: state.at[0, 3:9, x, z], first_send, first_recv)
-    first.start()
-    for c in range(2):
-        @pl.when(seg == c)
-        def _():
-            state[0, 3:9, OWN_X, rows_at(RIM * (1 - c), HZ + RIM)] = leaving[:, :, rows_at(RIM * c, HZ + RIM)]
-
+    for copy in table_loads:
+        copy.wait()
+    look_up(ids, tables, coefs)
     for m in range(2):
         @pl.when(seg == m)
         def _():
@@ -465,15 +468,15 @@
     cells = moment_cells.reshape(ENT // 128, 128)
     rows = drm_rows.reshape(ROWS // 128, 128)
     hbm = pl.BlockSpec(memory_space=pl.ANY)
-    smem = pl.BlockSpec(memory_space=pltpu.SMEM)
     dma = pltpu.SemaphoreType.DMA
     vmem = pltpu.VMEM
     return pl.pallas_call(
         functools.partial(kernel, n_sec, n_depth),
-        out_shape=jax.ShapeDtypeStruct(fields.shape, F32),
-        in_specs=[hbm, hbm, smem, smem, smem, hbm, hbm, hbm, hbm],
-        out_specs=hbm,
+        out_shape=pltpu.VMEM(fields.shape, F32),
+        in_specs=[hbm] * 9,
+        out_specs=pl.BlockSpec(memory_space=pltpu.VMEM),
         scratch_shapes=[
+            pltpu.SMEM((3, 16), F32),
             vmem((9, PX, GZ, CY), F32),
             vmem((PX, GZ, CY), I32),
             vmem((2, 9, PX, RZ, CY), F32),
@@ -495,7 +498,7 @@
             vmem((BUCKETS, 4, 128), F32),
             vmem((192, 2048), BF16),
             vmem((256, 2048), BF16),
-            dma((10,)),
+            dma((13,)),
             dma((4,)), dma((4,)),
             dma((8,)), dma((8,)),
             dma((8,)), dma((8,)),

time: 34.4 us -> 28.9 us (0.84); the launches traced: 33.7 us -> 28.7 us
  Pallas kernels: 32.1 us -> 28.1 us
  local copies, waits for them, and re-layouts: 1.58 us -> 0.66 us
    pallas_call x1, Pallas kernels: 32.1 us -> 28.1 us  [on_device(): pl.pallas_call(functools.partial(kernel, n_sec, n_depth), out_shape=pltpu...]
    unnamed x1, local copies, waits for them, and re-layouts: 1.58 us -> 0.66 us
where the time goes in v3:
time: 28.9 us; the launch traced here: 28.7 us
  Pallas kernels  28.1 us (97%)
  local copies, waits for them, and re-layouts  0.66 us (2%)
    pallas_call x1, Pallas kernels, on_device(): pl.pallas_call(functools.partial(kernel, n_sec, n_depth), out_shape=pltpu...  28.1 us
    unnamed x1, local copies, waits for them, and re-layouts  0.66 us

profile of v3, /device:TPU:31, one launch (start us, length us, event | category | flops | bytes accessed | tf_op | source)
XLA Modules:
  0.0 28.7 jit_solution(16903915964099030903)
XLA Ops:
  0.0 28.1 %shard_map.91 = f32[1,9,2,16,128]{4,3,2,1,0:T(8,128)S(1)} custom-call(f32[1,9,2,16,128]{4,3,2,1,0:T(8,128)} %fields.1, s32[1,2,16,128]{3,2,1,0:T(8,128)} %block_ids.1, f32[16]{0:T(128)} %buoyancy.1, f32[16]{0:T(128)} %lame_lambda.1, f32[16]{0:T(128)} %lame_mu.1, f32[6,1024]{1,0:T(8,128)} %moments.1, s32[8,128]{1,0:T(8,128)} %bitcast.4, s32[8,128]{1,0:T(8,128)} %bitcast.5, ...), custom_call_target="tpu_custom_call" | custom-call | tf_op jit(solution)/shard_map/pallas_call | solution.py:473
  28.1 0.7 %copy.11 = f32[1,9,2,16,128]{4,3,2,1,0:T(8,128)} copy(f32[1,9,2,16,128]{4,3,2,1,0:T(8,128)S(1)} %shard_map.91) | data formatting | bytes 294912

commit v4 on v3

--- a/solution.py
+++ b/solution.py
@@ -76,12 +76,19 @@
     return (cell >> 7) & 15, ((cell >> 11) << 7) | (cell & 127)
 
 
-def add_buckets(arrived, raw, leaving, lhs, rhs):
-    low_half = lax.broadcasted_iota(I32, (16, 128), 1) < CAP
+def by_distance(n_sec):
+    def hops(offset):
+        row, col = offset // 4, offset % 4
+        return min(row, n_sec // 4 - row) + min(col, 4 - col)
+
+    return sorted(range(1, n_sec), key=hops)
+
+
+def spread_buckets(arrived, batch, lhs, rhs):
+    low_half = lax.broadcasted_iota(I32, (8, 128), 1) < CAP
     values, cell = [], None
     for j in range(4):
-        rows = arrived[:, j, :]
-        a, b = rows[0:16], rows[16:32]
+        a, b = arrived[batch * 16:batch * 16 + 8, j, :], arrived[batch * 16 + 8:batch * 16 + 16, j, :]
         even = jnp.where(low_half, a, pltpu.roll(b, CAP, 1))
         if j < 3:
             values.append(even)
@@ -92,18 +99,16 @@
     parts = [split(value) for value in values]
     row16 = lax.broadcasted_iota(I32, (16, 128), 0)
     row256 = lax.broadcasted_iota(I32, (256, 128), 0)
-    for t in range(16):
-        at = slice(t * 128, (t + 1) * 128)
+    half = slice(batch * 1024, (batch + 1) * 1024)
+    for t in range(8):
+        at = slice(batch * 1024 + t * 128, batch * 1024 + (t + 1) * 128)
         mine = row16 == z[t:t + 1]
         rhs[:, at] = jnp.where(row256 == lane[t:t + 1], 1.0, 0.0).astype(BF16)
         for k, (high, low) in enumerate(parts):
             lhs[k * 16:(k + 1) * 16, at] = jnp.where(mine, high[t:t + 1], 0.0).astype(BF16)
             lhs[96 + k * 16:96 + (k + 1) * 16, at] = jnp.where(mine, low[t:t + 1], 0.0).astype(BF16)
-    sums = lax.dot_general(lhs[...], rhs[...], NT, preferred_element_type=F32)
-    sums = sums[0:96] + sums[96:192]
-    for k in range(6):
-        for x in range(CX):
-            leaving[k, x] = raw[k, x] + sums[k * 16:(k + 1) * 16, x * 128:(x + 1) * 128]
+    sums = lax.dot_general(lhs[:, half], rhs[:, half], NT, preferred_element_type=F32)
+    return sums[0:96] + sums[96:192]
 
 
 def count_rows(rows, counted, lhs, rhs):
@@ -274,17 +279,18 @@
 
     pl.semaphore_wait(barrier, expected)
 
-    def passed(j):
-        to = lax.rem(sec + j, n_sec)
+    offsets = by_distance(n_sec)
+
+    def passed(slot):
+        to = lax.rem(sec + offsets[slot - 1], n_sec)
         return remote(
-            bucket.at[lax.rem(to, 2) * 16 + to // 2], arrived.at[sec], all_send.at[j], all_recv.at[j], (to, depth, seg)
+            bucket.at[lax.rem(to, 2) * 16 + to // 2], arrived.at[slot], all_send.at[slot], all_recv.at[slot], (to, depth, seg)
         )
 
-    @pl.loop(0, n_sec - 1)
-    def _(t):
-        passed(1 + lax.rem(t + n_sec // 2 - 1, n_sec - 1)).start()
-
-    arrived[sec] = bucket[lax.rem(sec, 2) * 16 + sec // 2]
+    for slot in reversed(range(1, n_sec)):
+        passed(slot).start()
+
+    arrived[0] = bucket[lax.rem(sec, 2) * 16 + sec // 2]
 
     raw, raw_ids = Group(), Group()
     for q, (dx, dz) in enumerate(NEAR):
@@ -333,12 +339,18 @@
     pl.when(seg == 0)(own_stress.wait)
     pl.when(seg == 1)(partner_stress.wait_recv)
 
-    @pl.loop(1, n_sec)
-    def _(j):
-        come = lax.rem(sec + n_sec - j, n_sec)
-        remote(bucket.at[0], arrived.at[come], all_send.at[j], all_recv.at[j], (come, depth, seg)).wait_recv()
-
-    add_buckets(arrived, raw_stress, leaving, lhs, rhs)
+    for slot in range(1, min(16, n_sec)):
+        passed(slot).wait_recv()
+    near_sums = spread_buckets(arrived, 0, lhs, rhs)
+    for k in range(6):
+        for x in range(CX):
+            raw_stress[k, x] += near_sums[k * 16:(k + 1) * 16, x * 128:(x + 1) * 128]
+    for slot in range(16, n_sec):
+        passed(slot).wait_recv()
+    far_sums = spread_buckets(arrived, 1, lhs, rhs)
+    for k in range(6):
+        for x in range(CX):
+            leaving[k, x] = raw_stress[k, x] + far_sums[k * 16:(k + 1) * 16, x * 128:(x + 1) * 128]
     first = window(lambda z: leaving.at[:, :, z], lambda x, z: state.at[0, 3:9, x, z], first_send, first_recv)
     first.start()
     for c in range(2):
@@ -449,9 +461,8 @@
             hand_ids[c].wait_send()
             hand[c].wait_send()
 
-    @pl.loop(1, n_sec)
-    def _(j):
-        passed(j).wait_send()
+    for slot in range(1, n_sec):
+        passed(slot).wait_send()
 
     for c in range(2):
         @pl.when(seg == c)

time: 28.9 us -> 28.3 us (0.979)
  Pallas kernels: 28.1 us -> 27.5 us
    pallas_call x1, Pallas kernels: 28.1 us -> 27.5 us  [on_device(): pl.pallas_call(functools.partial(kernel, n_sec, n_depth), out_shape=pltpu...]
where the time goes in v4:
time: 28.3 us; the launch traced here: 28.2 us
  Pallas kernels  27.5 us (97%)
  local copies, waits for them, and re-layouts  0.66 us (2%)
    pallas_call x1, Pallas kernels, on_device(): pl.pallas_call(functools.partial(kernel, n_sec, n_depth), out_shape=pltpu...  27.5 us
    unnamed x1, local copies, waits for them, and re-layouts  0.66 us

profile of v4, /device:TPU:31, one launch (start us, length us, event | category | flops | bytes accessed | tf_op | source)
XLA Modules:
  0.0 28.2 jit_solution(12376423022532087647)
XLA Ops:
  0.0 27.5 %shard_map.91 = f32[1,9,2,16,128]{4,3,2,1,0:T(8,128)S(1)} custom-call(f32[1,9,2,16,128]{4,3,2,1,0:T(8,128)} %fields.1, s32[1,2,16,128]{3,2,1,0:T(8,128)} %block_ids.1, f32[16]{0:T(128)} %buoyancy.1, f32[16]{0:T(128)} %lame_lambda.1, f32[16]{0:T(128)} %lame_mu.1, f32[6,1024]{1,0:T(8,128)} %moments.1, s32[8,128]{1,0:T(8,128)} %bitcast.4, s32[8,128]{1,0:T(8,128)} %bitcast.5, ...), custom_call_target="tpu_custom_call" | custom-call | tf_op jit(solution)/shard_map/pallas_call | solution.py:484
  27.6 0.7 %copy.11 = f32[1,9,2,16,128]{4,3,2,1,0:T(8,128)} copy(f32[1,9,2,16,128]{4,3,2,1,0:T(8,128)S(1)} %shard_map.91) | data formatting | bytes 294912

commit v5 on v4

--- a/solution.py
+++ b/solution.py
@@ -237,6 +237,17 @@
     def there(dx, dz):
         return in_range(sec + dx, depth + dz, n_sec, n_depth)
 
+    offsets = by_distance(n_sec)
+    barrier = pltpu.get_barrier_semaphore()
+
+    def greet(offset):
+        to = (lax.rem(sec + offset, n_sec), depth, seg)
+        pl.semaphore_signal(barrier, inc=1, device_id=to, device_id_type=MESH)
+
+    for offset in reversed(offsets):
+        if offset not in (1, n_sec - 1):
+            greet(offset)
+
     loads = [load(0, owners, owner_v), load(1, cells, cells_v), load(2, moments, mom_v), load(3, rows, rows_v)]
     table_loads = [load(10 + k, table, tables.at[k]) for k, table in enumerate((buoyancy, lame_lambda, lame_mu))]
     for copy in loads + table_loads:
@@ -249,13 +260,9 @@
     if n_sec < BUCKETS:
         arrived[...] = jnp.zeros_like(arrived)
 
-    barrier = pltpu.get_barrier_semaphore()
     expected = jnp.int32(n_sec)
-
-    @pl.loop(1, n_sec)
-    def _(j):
-        pl.semaphore_signal(barrier, inc=1, device_id=(lax.rem(sec + j, n_sec), depth, seg), device_id_type=MESH)
-
+    greet(1)
+    greet(n_sec - 1)
     pl.semaphore_signal(barrier, inc=1, device_id=partner, device_id_type=MESH)
     for dx, dz in NEAR:
         if dz != 0:
@@ -278,8 +285,6 @@
     fill_buckets(owner_v, cells_v, mom_v, bucket, lhs, rhs)
 
     pl.semaphore_wait(barrier, expected)
-
-    offsets = by_distance(n_sec)
 
     def passed(slot):
         to = lax.rem(sec + offsets[slot - 1], n_sec)

time: 28.3 us -> 28.2 us (level)
  no operation moved by 1% of the time
where the time goes in v5:
time: 28.2 us; the launch traced here: 28.1 us
  Pallas kernels  27.4 us (97%)
  local copies, waits for them, and re-layouts  0.66 us (2%)
    pallas_call x1, Pallas kernels, on_device(): pl.pallas_call(functools.partial(kernel, n_sec, n_depth), out_shape=pltpu...  27.4 us
    unnamed x1, local copies, waits for them, and re-layouts  0.66 us

profile of v5, /device:TPU:31, one launch (start us, length us, event | category | flops | bytes accessed | tf_op | source)
XLA Modules:
  0.0 28.1 jit_solution(7963036949526531931)
XLA Ops:
  0.0 27.4 %shard_map.91 = f32[1,9,2,16,128]{4,3,2,1,0:T(8,128)S(1)} custom-call(f32[1,9,2,16,128]{4,3,2,1,0:T(8,128)} %fields.1, s32[1,2,16,128]{3,2,1,0:T(8,128)} %block_ids.1, f32[16]{0:T(128)} %buoyancy.1, f32[16]{0:T(128)} %lame_lambda.1, f32[16]{0:T(128)} %lame_mu.1, f32[6,1024]{1,0:T(8,128)} %moments.1, s32[8,128]{1,0:T(8,128)} %bitcast.4, s32[8,128]{1,0:T(8,128)} %bitcast.5, ...), custom_call_target="tpu_custom_call" | custom-call | tf_op jit(solution)/shard_map/pallas_call | solution.py:489
  27.4 0.7 %copy.11 = f32[1,9,2,16,128]{4,3,2,1,0:T(8,128)} copy(f32[1,9,2,16,128]{4,3,2,1,0:T(8,128)S(1)} %shard_map.91) | data formatting | bytes 294912

commit v6 on v5

--- a/solution.py
+++ b/solution.py
@@ -317,15 +317,16 @@
     pl.when(seg == 0)(partner_stress.start)
     raw.start()
 
-    def window(source, target, send, recv):
+    def window(source, target, send, recv, trim=False):
         group = Group()
         for c in range(2):
             dz = 1 - 2 * c
             for q, (dx, goes) in enumerate(((-1, 0), (1, 0), (0, dz), (-1, dz), (1, dz))):
+                less = 1 if trim and dx == -1 and c == (0 if goes == 0 else 1) else 0
                 if goes == 0:
-                    from_z, to_z = rows_at(RIM * c, HZ + RIM), rows_at(RIM * (1 - c), HZ + RIM)
+                    from_z, to_z = rows_at(RIM * c, HZ + RIM - less), rows_at(RIM * (1 - c), HZ + RIM - less)
                 else:
-                    from_z, to_z = rows_at((CZ - RIM) * (1 - c), RIM), rows_at((HZ + RIM) * c, RIM)
+                    from_z, to_z = rows_at((CZ - RIM) * (1 - c), RIM - less), rows_at((HZ + RIM) * c, RIM - less)
                 group.add(
                     remote(source(from_z), target(beside(dx), to_z), send.at[q], recv.at[q], (sec + dx, depth + goes, seg)),
                     jnp.logical_and(there(dx, goes), seg == c), jnp.logical_and(there(-dx, -goes), seg == c),
@@ -356,7 +357,7 @@
     for k in range(6):
         for x in range(CX):
             leaving[k, x] = raw_stress[k, x] + far_sums[k * 16:(k + 1) * 16, x * 128:(x + 1) * 128]
-    first = window(lambda z: leaving.at[:, :, z], lambda x, z: state.at[0, 3:9, x, z], first_send, first_recv)
+    first = window(lambda z: leaving.at[:, :, z], lambda x, z: state.at[0, 3:9, x, z], first_send, first_recv, True)
     first.start()
     for c in range(2):
         @pl.when(seg == c)
@@ -417,10 +418,14 @@
             to_left[m, k] = state[m, k, lo]
 
     second = Group()
-    z = rows_at(2, RZ - 4)
-    for q, (dx, src, dst) in enumerate(((1, to_right, from_left), (-1, to_left, from_right))):
+    sent = (
+        (1, to_right, from_left, rows_at(0, 6), rows_at(RIM - 1, HZ + 3)),
+        (-1, to_left, from_right, rows_at(3, 6), rows_at(RIM - 2, HZ + 3)),
+        (-1, to_left, from_right, rows_at(0, 3), rows_at(RIM - 1, HZ + 1)),
+    )
+    for q, (dx, src, dst, kinds, z) in enumerate(sent):
         second.add(
-            remote(src.at[:, :, z], dst.at[:, :, z], second_send.at[q], second_recv.at[q], (sec + dx, depth, seg)),
+            remote(src.at[:, kinds, z], dst.at[:, kinds, z], second_send.at[q], second_recv.at[q], (sec + dx, depth, seg)),
             there(dx, 0), there(-dx, 0),
         )
     second.start()
@@ -428,17 +433,17 @@
 
     @pl.when(there(-1, 0))
     def _():
+        z = sent[0][4]
         for m in range(2):
             for k, part in enumerate((0, 1, 2, 3, 7, 8)):
-                state[m, part, lo - 1] = from_left[m, k]
+                state[m, part, lo - 1, z] = from_left[m, k, z]
 
     @pl.when(there(1, 0))
     def _():
         for m in range(2):
-            for k in range(3):
-                state[m, k, hi + 2] = from_right[m, k]
-            for k in range(3, 9):
-                state[m, k, hi + 1] = from_right[m, k]
+            for k in range(9):
+                z = sent[2][4] if k < 3 else sent[1][4]
+                state[m, k, hi + 2 if k < 3 else hi + 1, z] = from_right[m, k, z]
 
     velocity(state, coefs, counts, (lo, hi + 1))
     stress(state, coefs, range(lo - 1, hi + 2))
@@ -521,7 +526,7 @@
             dma((5,)), dma((5,)),
             dma((BUCKETS,)), dma((BUCKETS,)),
             dma((5,)), dma((5,)),
-            dma((2,)), dma((2,)),
+            dma((3,)), dma((3,)),
         ],
         compiler_params=pltpu.CompilerParams(collective_id=0, has_side_effects=True),
     )(fields, block_ids, buoyancy, lame_lambda, lame_mu, moments, owners, cells, rows)

time: 28.2 us -> 28.1 us (level)
  no operation moved by 1% of the time
where the time goes in v6:
time: 28.1 us; the launch traced here: 28 us
  Pallas kernels  27.3 us (97%)
  local copies, waits for them, and re-layouts  0.66 us (2%)
    pallas_call x1, Pallas kernels, on_device(): pl.pallas_call(functools.partial(kernel, n_sec, n_depth), out_shape=pltpu...  27.3 us
    unnamed x1, local copies, waits for them, and re-layouts  0.66 us

profile of v6, /device:TPU:31, one launch (start us, length us, event | category | flops | bytes accessed | tf_op | source)
XLA Modules:
  0.0 28.0 jit_solution(10508894544764291188)
XLA Ops:
  0.0 27.3 %shard_map.91 = f32[1,9,2,16,128]{4,3,2,1,0:T(8,128)S(1)} custom-call(f32[1,9,2,16,128]{4,3,2,1,0:T(8,128)} %fields.1, s32[1,2,16,128]{3,2,1,0:T(8,128)} %block_ids.1, f32[16]{0:T(128)} %buoyancy.1, f32[16]{0:T(128)} %lame_lambda.1, f32[16]{0:T(128)} %lame_mu.1, f32[6,1024]{1,0:T(8,128)} %moments.1, s32[8,128]{1,0:T(8,128)} %bitcast.4, s32[8,128]{1,0:T(8,128)} %bitcast.5, ...), custom_call_target="tpu_custom_call" | custom-call | tf_op jit(solution)/shard_map/pallas_call | solution.py:494
  27.3 0.7 %copy.11 = f32[1,9,2,16,128]{4,3,2,1,0:T(8,128)} copy(f32[1,9,2,16,128]{4,3,2,1,0:T(8,128)S(1)} %shard_map.91) | data formatting | bytes 294912
